TPU v7x, 32 devices: a whole 2x2x4 slice. The times are simulated.
32 devices in a mesh: seq: 16 (over z, x, core), tp: 2 (over y).
Axes of the slice: x: 2, y: 2, z: 4, core: 2. Of those that a mesh axis runs over, the one named last changes fastest.
Arguments:
- tokens: bfloat16 [2048, 2048], P('seq', 'tp'), may hold values from -6 to 6
- attn_gain: bfloat16 [2048], replicated, may hold values from 0.25 to 1.75
- w_query: bfloat16 [2048, 2048], P(None, 'tp'), may hold values from -1 to 9
- w_key: bfloat16 [2048, 2048], P(None, 'tp'), may hold values from -0.125 to 0.125
- w_value: bfloat16 [2048, 2048], P(None, 'tp'), may hold values from -0.125 to 0.125
- w_out: bfloat16 [2048, 2048], P('tp'), may hold values from -0.5 to 0.5
- prefix_keys: bfloat16 [512, 2048], P('seq', 'tp'), may hold values from -6 to 6
- prefix_values: bfloat16 [512, 2048], P('seq', 'tp'), may hold values from -6 to 6
- shard_group: int32 [16], replicated, may hold values from 0 to 1, as said below
- request_group: int32 [8], replicated, may hold values from 0 to 1, as said below
- lengths: int32 [8], replicated, may hold values from 1 to 512, 2048 in all
- moe_gain: bfloat16 [2048], replicated, may hold values from 0.25 to 1.75
- w_router: bfloat16 [2048, 16], replicated, may hold values from -1 to 8
- w_gate: bfloat16 [16, 2048, 1024], P('seq', None, 'tp'), may hold values from -0.125 to 0.125
- w_up: bfloat16 [16, 2048, 1024], P('seq', None, 'tp'), may hold values from -0.125 to 0.125
- w_down: bfloat16 [16, 1024, 2048], P('seq', 'tp'), may hold values from -3 to 3
- routes: int32 [2048, 8], P('seq'), may hold values from 0 to 15, all different within a row; in each aligned block of 128 rows (0 to 127, 128 to 255, ...) at most 96 rows name the same one
- final_gain: bfloat16 [2048], P('tp'), may hold values from 0.25 to 1.75
- w_head: bfloat16 [2048, 50304], P('tp', 'seq'), may hold values from -2 to 9
Outputs:
- hidden: bfloat16 [2048, 2048], P('seq', 'tp')
- log_probs: float32 [8, 50304], P(None, 'seq')
Inputs may be any that keep to these rules, and one draw needn't show every extreme that they name: `shard_group`: exactly half of the 16 cache shards belong to each group. `request_group`: exactly half of the requests belong to each group. The lengths sum to 2048; the largest is exactly 512. `routes`: among the rows of one device no expert is named more than 96 times, a bound that some block reaches.
All inputs are finite; a program needn't handle non-finite values.
Results may differ from a plain program's by a relative error of at most 0.017.
The roundings to bfloat16 on the way count: a program that leaves them out, or rounds other values in their place, can miss the bound.
Values may be sent and summed in bfloat16 or wider, within the bound.
A program may use at most 128 MiB of HBM per device.

v0:
```python
import jax
import jax.numpy as jnp
from jax import lax
from jax.sharding import PartitionSpec as P

HD = 128
SPAN = 4


EPS = 1e-05
NEGATIVE = -1e30


def from_behind(value, axis, steps):
    count = lax.axis_size(axis)
    leading, last = (max(0, -steps), min(count, count - steps))
    return lax.ppermute(value, axis, [(source, source + steps) for source in range(leading, last)])


def normalize(rows, gain):
    inv = lax.rsqrt(jnp.mean(rows * rows, -1, keepdims=True) + EPS)
    return rows * inv * gain.astype(jnp.float32)


def rotate(vectors, position):
    half = vectors.shape[-1] // 2
    freq = 10000.0 ** (-jnp.arange(half).astype(jnp.float32) / half)
    angle = position[:, None] * freq[None, :]
    cosine = jnp.cos(angle)[:, None, :]
    sine = jnp.sin(angle)[:, None, :]
    first = vectors[..., :half]
    second = vectors[..., half:]
    return jnp.concatenate([first * cosine - second * sine, second * cosine + first * sine], -1)


def request_of(index, ends):
    return jnp.sum((index[:, None] >= ends[None, :]).astype(jnp.int32), 1)


def lookup(selector, table):
    hit = selector[:, None] == jnp.arange(table.shape[0])[None, :]
    return jnp.sum(jnp.where(hit, table[None, :], 0), 1)


def attend(carry, query, keys, values, allowed):
    best, total, accum = carry
    heads = query.shape[1]
    keys = keys.reshape(keys.shape[0], heads, -1)
    values = values.reshape(values.shape[0], heads, -1)
    scale = query.shape[-1] ** (-0.5)
    scores = jnp.einsum("thd,khd->htk", query, keys, preferred_element_type=jnp.float32) * scale
    scores = jnp.where(allowed[None], scores, NEGATIVE)
    top = jnp.maximum(best, jnp.max(scores, -1))
    factor = jnp.exp(best - top)
    weights = jnp.where(allowed[None], jnp.exp(scores - top[..., None]), 0.0)
    total = factor * total + jnp.sum(weights, -1)
    accum = factor[..., None] * accum + jnp.einsum(
        "htk,khd->htd", weights.astype(jnp.bfloat16), values, preferred_element_type=jnp.float32
    )
    return (top, total, accum)


def on_device(
    tokens,
    attn_gain,
    w_query,
    w_key,
    w_value,
    w_out,
    prefix_keys,
    prefix_values,
    shard_group,
    request_group,
    lengths,
    moe_gain,
    w_router,
    w_gate,
    w_up,
    w_down,
    routes,
    final_gain,
    w_head,
):
    f32 = jnp.float32
    bf16 = jnp.bfloat16
    seq_index = lax.axis_index("seq")
    tp_index = lax.axis_index("tp")
    seq_count = lax.axis_size("seq")
    tp_count = lax.axis_size("tp")
    tok_dev = tokens.shape[0]
    width_part = tokens.shape[1]
    shard_rows = prefix_keys.shape[0]
    prefix_length = shard_rows * seq_count // 2
    full_x = lax.all_gather(tokens, "tp", axis=1, tiled=True)
    width = full_x.shape[1]
    normed = normalize(full_x.astype(f32), attn_gain).astype(bf16)
    heads = w_query.shape[1] // HD
    ends = jnp.cumsum(lengths)
    starts = ends - lengths
    local_index = seq_index * tok_dev + jnp.arange(tok_dev)
    own_request = request_of(local_index, ends)
    own_start = lookup(own_request, starts)
    own_group = lookup(own_request, request_group)
    position = (prefix_length + local_index - own_start).astype(f32)
    query = rotate(
        jnp.dot(normed, w_query, preferred_element_type=f32).reshape(tok_dev, heads, HD), position
    ).astype(bf16)
    key_rows = rotate(
        jnp.dot(normed, w_key, preferred_element_type=f32).reshape(tok_dev, heads, HD), position
    ).astype(bf16)
    key_rows = key_rows.reshape(tok_dev, heads * HD)
    value_rows = jnp.dot(normed, w_value, preferred_element_type=f32).astype(bf16)
    start_state = (
        jnp.full((heads, tok_dev), NEGATIVE, f32),
        jnp.zeros((heads, tok_dev), f32),
        jnp.zeros((heads, tok_dev, HD), f32),
    )
    pieces = (
        lax.all_gather(prefix_keys, "seq", axis=0, tiled=True),
        lax.all_gather(prefix_values, "seq", axis=0, tiled=True),
    )
    count = pieces[0].shape[0]
    shard_ids = jnp.arange(count) // shard_rows
    key_group = lookup(shard_ids, shard_group)
    fold_allowed = own_group[:, None] == key_group[None, :]
    state = attend(start_state, query, pieces[0], pieces[1], fold_allowed)
    own_allowed = (own_request[:, None] == own_request[None, :]) & (
        local_index[None, :] <= local_index[:, None]
    )
    state = attend(state, query, key_rows, value_rows, own_allowed)
    both_rows = jnp.stack([key_rows, value_rows])
    moving = both_rows
    for step in range(1, SPAN + 1):
        moving = from_behind(moving, "seq", 1)
        key_index = (seq_index - step) * tok_dev + jnp.arange(tok_dev)
        key_request = request_of(key_index, ends)
        allowed = (key_index >= 0)[None, :] & (own_request[:, None] == key_request[None, :])
        state = attend(state, query, moving[0], moving[1], allowed)
    best, total, accum = state
    attended = (accum / total[..., None]).astype(bf16)
    attended = jnp.transpose(attended, (1, 0, 2)).reshape(tok_dev, heads * HD)
    mixed = jnp.dot(attended, w_out, preferred_element_type=f32)
    attn_part = lax.psum_scatter(mixed, "tp", scatter_dimension=1, tiled=True)
    resid = (tokens.astype(f32) + attn_part).astype(bf16)
    resid_f = resid.astype(f32)
    squares = lax.psum(jnp.sum(resid_f * resid_f, -1), "tp")
    gain_part = lax.dynamic_slice_in_dim(moe_gain, tp_index * width_part, width_part, 0).astype(f32)
    scaled = (resid_f * lax.rsqrt(squares / width + EPS)[:, None] * gain_part).astype(bf16)
    moe_in = lax.all_gather(scaled, "tp", axis=1, tiled=True)
    experts = w_router.shape[1]
    topk = routes.shape[1]
    probs = jax.nn.softmax(jnp.dot(moe_in, w_router, preferred_element_type=f32), -1)
    flat = routes.reshape(-1)
    hits = (flat[:, None] == jnp.arange(experts)[None, :]).astype(jnp.int32)
    rank = jnp.sum((jnp.cumsum(hits, 0) - hits) * hits, 1)
    capacity = min(tok_dev, tp_count * max(1, 3 * tok_dev * topk // (2 * experts * tp_count)))
    target = flat * capacity + rank
    route_weight = jnp.sum(hits.reshape(tok_dev, topk, experts).astype(f32) * probs[:, None, :], -1)
    repeated = jnp.repeat(moe_in, topk, axis=0)
    outgoing = (
        jnp.zeros((experts * capacity, width), bf16)
        .at[target]
        .set(repeated)
        .reshape(experts, capacity, width)
    )
    arrived = lax.all_to_all(outgoing, "seq", split_axis=0, concat_axis=0, tiled=True)
    sources = arrived.shape[0]
    count = arrived.shape[1]
    rows = arrived.reshape(sources * count, width)
    gate = jnp.dot(rows, w_gate[0], preferred_element_type=f32)
    up = jnp.dot(rows, w_up[0], preferred_element_type=f32)
    act = (jax.nn.silu(gate) * up).astype(bf16)
    partial_out = jnp.dot(act, w_down[0], preferred_element_type=f32).reshape(sources, count, width)
    summed = lax.psum_scatter(partial_out, "tp", scatter_dimension=2, tiled=True).astype(bf16)
    returned = lax.all_to_all(summed, "seq", split_axis=0, concat_axis=0, tiled=True)
    picked = returned.reshape(experts * capacity, width_part)[target].reshape(
        tok_dev, topk, width_part
    )
    moe_part = jnp.sum(picked.astype(f32) * route_weight[:, :, None], 1)
    hidden = (resid.astype(f32) + moe_part).astype(bf16)
    hidden_f = hidden.astype(f32)
    final_sq = lax.psum(jnp.sum(hidden_f * hidden_f, -1), "tp")
    final = (hidden_f * lax.rsqrt(final_sq / width + EPS)[:, None] * final_gain.astype(f32)).astype(
        bf16
    )
    last_hit = ((ends - 1)[:, None] == local_index[None, :]).astype(bf16)
    chosen = jnp.dot(last_hit, final, preferred_element_type=f32)
    chosen = lax.psum(chosen, "seq").astype(bf16)
    logits = lax.psum(jnp.dot(chosen, w_head, preferred_element_type=f32), "tp")
    peak_logit = lax.pmax(jnp.max(logits, -1), "seq")
    total_exp = lax.psum(jnp.sum(jnp.exp(logits - peak_logit[:, None]), -1), "seq")
    log_probs = logits - peak_logit[:, None] - jnp.log(total_exp)[:, None]
    return (hidden, log_probs)


def solution(mesh):
    in_specs = (
        P("seq", "tp"),
        P(),
        P(None, "tp"),
        P(None, "tp"),
        P(None, "tp"),
        P("tp", None),
        P("seq", "tp"),
        P("seq", "tp"),
        P(),
        P(),
        P(),
        P(),
        P(),
        P("seq", None, "tp"),
        P("seq", None, "tp"),
        P("seq", "tp", None),
        P("seq", None),
        P("tp"),
        P("tp", "seq"),
    )
    out_specs = (P("seq", "tp"), P(None, "seq"))
    return jax.shard_map(
        on_device, mesh=mesh, in_specs=in_specs, out_specs=out_specs, check_vma=False
    )
```

profile of v0, /device:TPU:0, one launch (start us, length us, event | category | flops | bytes accessed | tf_op | source)
XLA Modules:
  0.0 712.6 jit_solution(14022461125076559088)
XLA Ops:
  8.0 10.2 %all_gather.12 = bf16[128,2048]{1,0:T(8,128)(2,1)S(1)} all-gather(bf16[128,1024]{1,0:T(8,128)(2,1)} %param.19), channel_id=1, replica_groups=mesh['seq'=16,'tp'=2] {'tp'}, dimensions={1}, use_global_device_ids=true | all-gather | bytes 786432 | tf_op jit(solution)/shard_map/all_gather | solution.py:94
  19.1 4.0 fusion.119
  30.0 2.9 convolution_convert_fusion
  33.9 2.1 collective-permute-start
  36.1 3.1 convolution_bitcast_fusion.6
  40.9 7.3 %collective-permute-start.1 = (bf16[2,128,1024]{2,1,0:T(8,128)(2,1)}, bf16[2,128,1024]{2,1,0:T(8,128)(2,1)}, u32[]{:S(2)}, u32[]{:S(2)}) collective-permute-start(bf16[2,128,1024]{2,1,0:T(8,128)(2,1)} %collective-permute-done), channel_id=1, source_target_pairs={{0,2},{2,4},{4,6},{6,8},{8,10},{10,12},{12,14},{14,16},{16,18},{18... | collective-permute-start | bytes 1572872 | tf_op jit(solution)/shard_map/ppermute | solution.py:17
  50.1 1.8 fusion.129
  51.9 7.1 collective-permute-start.2
  59.9 1.8 copy.142
  61.7 1.8 fusion.128
  64.2 1.8 copy.143
  66.0 2.7 fusion.134
  68.7 1.8 fusion.127
  71.2 1.8 copy.144
  73.0 4.4 collective-permute-start.3
  77.4 2.6 fusion.133
  80.1 2.3 copy.106
  82.4 10.5 %all-gather.5.cloned.1.call-done = bf16[512,1024]{1,0:T(8,128)(2,1)} async-done(((bf16[32,1024]{1,0:T(8,128)(2,1)}), bf16[512,1024]{1,0:T(8,128)(2,1)}) %all-gather.5.cloned.1.call-update) | async-done | bytes 1048592 | tf_op jit(solution)/shard_map/all_gather | solution.py:120
  92.9 2.3 copy.117
  95.2 3.7 fusion.11
  98.9 1.8 fusion.126
  101.4 1.8 copy.145
  103.3 1.4 fusion.132
  105.4 2.3 fusion.12
  110.9 1.5 copy-done.2
  112.4 1.7 fusion.138
  114.5 4.5 reduce-window.18
  119.7 14.9 %reduce-scatter.3.cloned.1.call-done = f32[128,1024]{1,0:T(8,128)} async-done(((f32[128,2048]{1,0:T(8,128)}), f32[128,1024]{1,0:T(8,128)}) %reduce-scatter.3.cloned.1.call-update) | async-done | bytes 524304 | tf_op jit(solution)/shard_map/reduce_scatter | solution.py:143
  135.9 4.9 psum.35
  141.0 7.5 %all_gather.15 = bf16[128,2048]{1,0:T(8,128)(2,1)S(1)} all-gather(bf16[128,1024]{1,0:T(8,128)(2,1)S(1)} %fusion.46), channel_id=1, replica_groups=mesh['seq'=16,'tp'=2] {'tp'}, dimensions={1}, use_global_device_ids=true | all-gather | bytes 786432 | tf_op jit(solution)/shard_map/all_gather | solution.py:149
  148.5 10.2 %scatter_custom_fusion = bf16[1536,2048]{1,0:T(8,128)(2,1)} fusion(s32[1024]{0:T(1024)S(1)} %bitcast.248, bf16[]{:T(256)} %constant.87.clone.1, bf16[128,2048]{1,0:T(8,128)(2,1)S(1)} %all_gather.15), kind=kCustom, calls=%fused_computation.4 | custom fusion | bytes 6815746 | tf_op jit(solution)/shard_map/scatter | solution.py:163
  158.7 142.9 %all_to_all.10 = bf16[16,96,2048]{2,1,0:T(8,128)(2,1)S(1)} all-to-all(bf16[16,96,2048]{2,1,0:T(8,128)(2,1)} %bitcast.226), channel_id=1, replica_groups=mesh['seq'=16,'tp'=2] {'seq'}, dimensions={0} | all-to-all | bytes 12582912 | tf_op jit(solution)/shard_map/all_to_all | solution.py:166
  301.6 3.5 fusion.8
  305.1 3.9 fusion.4
  309.1 6.4 fusion.5
  315.5 144.5 %reduce-scatter.5.cloned.1.call-done = f32[16,96,1024]{2,1,0:T(8,128)} async-done(((f32[16,96,2048]{2,1,0:T(8,128)}), f32[16,96,1024]{2,1,0:T(8,128)}) %reduce-scatter.5.cloned.1.call-update) | async-done | bytes 6291472 | tf_op jit(solution)/shard_map/reduce_scatter | solution.py:174
  460.0 5.0 convert_element_type.163
  465.0 5.8 all-to-all-start.1
  471.6 58.6 %all-to-all-done.1 = bf16[16,96,1024]{2,1,0:T(8,128)(2,1)} async-done(((bf16[16,96,1024]{2,1,0:T(8,128)(2,1)}), bf16[16,96,1024]{2,1,0:T(8,128)(2,1)}, u32[]{:S(2)}, u32[]{:S(2)}) %all-to-all-start.1) | async-done | bytes 3145760 | tf_op jit(solution)/shard_map/all_to_all | solution.py:175
  530.2 8.3 %gather_fusion = bf16[1024,1024]{1,0:T(8,128)(2,1)} fusion(bf16[1536,1024]{1,0:T(8,128)(2,1)} %bitcast.43, s32[1024]{0:T(1024)S(1)} %broadcast_clamp_fusion), kind=kCustom, calls=%fused_computation | custom fusion | bytes 4198400 | tf_op jit(solution)/shard_map/gather | solution.py:176
  538.6 2.9 fusion
  541.7 4.9 psum.36
  546.9 70.3 %psum.37 = bf16[8,1024]{1,0:T(8,128)(2,1)S(1)} all-reduce(f32[8,1024]{1,0:T(8,128)S(1)} %fusion.63), channel_id=1, replica_groups=mesh['seq'=16,'tp'=2] {'seq'}, use_global_device_ids=true, to_apply=%region_36.37 | all-reduce | flops 8192 | bytes 49152 | tf_op jit(solution)/shard_map/psum | solution.py:188
  617.2 5.2 fusion.139
  622.5 17.5 %all-reduce.2.cloned.1.call-done = f32[8,3144]{1,0:T(8,128)} async-done(((f32[8,3144]{1,0:T(8,128)}), f32[8,3144]{1,0:T(8,128)}) %all-reduce.2.cloned.1.call-update) | async-done | bytes 100624 | tf_op jit(solution)/shard_map/psum | solution.py:189
  641.0 32.9 %pmax.7 = f32[8]{0:T(128)S(1)} all-reduce(f32[8]{0:T(128)S(1)} %reduce_max.94), channel_id=1, replica_groups=mesh['seq'=16,'tp'=2] {'seq'}, use_global_device_ids=true, to_apply=%region_39.40 | all-reduce | flops 8 | bytes 64 | tf_op jit(solution)/shard_map/pmax | solution.py:190
  675.0 29.5 %psum.39 = f32[8]{0:T(128)S(1)} all-reduce(f32[8]{0:T(128)S(1)} %exponential_reduce_fusion), channel_id=1, replica_groups=mesh['seq'=16,'tp'=2] {'seq'}, use_global_device_ids=true, to_apply=%region_41.42 | all-reduce | flops 8 | bytes 64 | tf_op jit(solution)/shard_map/psum | solution.py:191
  704.5 1.6 subtract_subtract_fusion
  (181 shorter events, 25.6 us)
Async XLA Ops:
  7.2 301.9 %copy-start = (bf16[1,512,2048]{2,1,0:T(8,128)(2,1)S(1)}, bf16[1,512,2048]{2,1,0:T(8,128)(2,1)}, u32[]{:S(2)}) copy-start(bf16[1,512,2048]{2,1,0:T(8,128)(2,1)} %param.34) | copy-start | bytes 6291460
  7.2 72.9 %all-gather.3.cloned.1.call-start = ((), (), s32[]{:S(2)}) async-start(), calls=%async_computation.4 | async-start | bytes 1114112 | tf_op jit(solution)/shard_map/all_gather | solution.py:119
  7.9 85.0 %all-gather.5.cloned.1.call-start = ((), (), s32[]{:S(2)}) async-start(), calls=%async_computation.5 | async-start | bytes 1114112 | tf_op jit(solution)/shard_map/all_gather | solution.py:120
  19.1 7.0 copy-start.38
  19.1 8.3 %copy-start.36 = (s32[8]{0:T(128)S(1)}, s32[8]{0:T(128)}, u32[]{:S(2)}) copy-start(s32[8]{0:T(128)} %param.28) | copy-start | bytes 100
  26.3 3.6 copy-start.26
  26.9 3.0 copy-start.24
  33.9 7.0 collective-permute-start
  36.0 98.7 %reduce-scatter.3.cloned.1.call-start = ((), (), s32[]{:S(2)}) async-start(), calls=%async_computation.6 | async-start | bytes 1572864 | tf_op jit(solution)/shard_map/reduce_scatter | solution.py:143
  36.1 3.5 copy-start.25
  36.1 3.5 copy-start.27
  36.1 3.5 copy-start.30
  36.1 3.5 copy-start.31
  36.1 3.5 copy-start.32
  36.1 3.5 copy-start.33
  36.1 4.3 copy-start.37
  39.2 1.5 copy-start.29
  40.7 18.2 %copy-start.15 = (pred[128,128]{0,1:T(8,128)(4,1)S(1)}, pred[128,128]{0,1:T(8,128)(4,1)}, u32[]{:S(2)}) copy-start(pred[128,128]{0,1:T(8,128)(4,1)} %get-tuple-element.46) | copy-start | bytes 49156
  40.9 11.0 %collective-permute-start.1 = (bf16[2,128,1024]{2,1,0:T(8,128)(2,1)}, bf16[2,128,1024]{2,1,0:T(8,128)(2,1)}, u32[]{:S(2)}, u32[]{:S(2)}) collective-permute-start(bf16[2,128,1024]{2,1,0:T(8,128)(2,1)} %collective-permute-done), channel_id=1, source_target_pairs={{0,2},{2,4},{4,6},{6,8},{8,10},{10,12},{12,14},{14,16},{16,18},{18... | collective-permute-start | bytes 1572872 | tf_op jit(solution)/shard_map/ppermute | solution.py:17
  49.2 16.9 %copy-start.14 = (pred[128,128]{0,1:T(8,128)(4,1)S(1)}, pred[128,128]{0,1:T(8,128)(4,1)}, u32[]{:S(2)}) copy-start(pred[128,128]{0,1:T(8,128)(4,1)} %get-tuple-element.47) | copy-start | bytes 49156
  51.9 16.8 %collective-permute-start.2 = (bf16[2,128,1024]{2,1,0:T(8,128)(2,1)}, bf16[2,128,1024]{2,1,0:T(8,128)(2,1)}, u32[]{:S(2)}, u32[]{:S(2)}) collective-permute-start(bf16[2,128,1024]{2,1,0:T(8,128)(2,1)} %collective-permute-done.1), channel_id=1, source_target_pairs={{0,2},{2,4},{4,6},{6,8},{8,10},{10,12},{12,14},{14,16},{16,18},{18... | collective-permute-start | bytes 1572872 | tf_op jit(solution)/shard_map/ppermute | solution.py:17
  59.9 17.6 %copy-start.13 = (pred[128,128]{0,1:T(8,128)(4,1)S(1)}, pred[128,128]{0,1:T(8,128)(4,1)}, u32[]{:S(2)}) copy-start(pred[128,128]{0,1:T(8,128)(4,1)} %get-tuple-element.48) | copy-start | bytes 49156
  73.0 25.9 %collective-permute-start.3 = (bf16[2,128,1024]{2,1,0:T(8,128)(2,1)}, bf16[2,128,1024]{2,1,0:T(8,128)(2,1)}, u32[]{:S(2)}, u32[]{:S(2)}) collective-permute-start(bf16[2,128,1024]{2,1,0:T(8,128)(2,1)} %collective-permute-done.2), channel_id=1, source_target_pairs={{0,2},{2,4},{4,6},{6,8},{8,10},{10,12},{12,14},{14,16},{16,18},{18... | collective-permute-start | bytes 1572872 | tf_op jit(solution)/shard_map/ppermute | solution.py:17
  95.2 8.1 %copy-start.16 = (pred[128,128]{0,1:T(8,128)(4,1)S(1)}, pred[128,128]{0,1:T(8,128)(4,1)}, u32[]{:S(2)}) copy-start(pred[128,128]{0,1:T(8,128)(4,1)} %get-tuple-element.49) | copy-start | bytes 49156
  103.2 4.7 copy-start.3
  103.2 4.8 copy-start.4
  103.2 5.1 copy-start.18
  103.2 5.1 copy-start.19
  103.2 5.1 copy-start.21
  103.2 5.1 copy-start.22
  103.2 5.1 copy-start.23
  103.2 5.1 copy-start.1
  103.2 5.1 copy-start.9
  109.2 1.2 copy-start.8
  110.2 2.2 copy-start.2
  112.4 1.8 copy-start.20
  112.4 7.2 %copy-start.35 = (bf16[2048]{0:T(1024)(128)(2,1)S(1)}, bf16[2048]{0:T(1024)(128)(2,1)}, u32[]{:S(2)}) copy-start(bf16[2048]{0:T(1024)(128)(2,1)} %param.30) | copy-start | bytes 12292
  112.4 22.3 %copy-start.10 = (bf16[128,1024]{1,0:T(8,128)(2,1)S(1)}, bf16[128,1024]{1,0:T(8,128)(2,1)}, u32[]{:S(2)}) copy-start(bf16[128,1024]{1,0:T(8,128)(2,1)} %param.19) | copy-start | bytes 786436
  114.1 345.9 %reduce-scatter.5.cloned.1.call-start = ((), (), s32[]{:S(2)}) async-start(), calls=%async_computation.7 | async-start | bytes 18874368 | tf_op jit(solution)/shard_map/reduce_scatter | solution.py:174
  158.7 142.9 %copy-start.40 = (bf16[1,2048,512]{2,1,0:T(8,128)(2,1)S(1)}, bf16[1,2048,512]{2,1,0:T(8,128)(2,1)}, u32[]{:S(2)}) copy-start(bf16[1,2048,512]{2,1,0:T(8,128)(2,1)} %param.32) | copy-start | bytes 6291460
  301.6 3.5 copy-start.41
  465.0 6.1 copy-start.34
  465.0 6.1 copy-start.17
  465.0 65.2 %all-to-all-start.1 = ((bf16[16,96,1024]{2,1,0:T(8,128)(2,1)}), bf16[16,96,1024]{2,1,0:T(8,128)(2,1)}, u32[]{:S(2)}, u32[]{:S(2)}) async-start(bf16[16,96,1024]{2,1,0:T(8,128)(2,1)} %convert_element_type.163), calls=%async_computation.3 | async-start | bytes 6291456 | tf_op jit(solution)/shard_map/all_to_all | solution.py:175
  470.8 169.1 %all-reduce.2.cloned.1.call-start = ((), (), s32[]{:S(2)}) async-start(), calls=%async_computation.8 | async-start | bytes 204800 | tf_op jit(solution)/shard_map/psum | solution.py:189
  538.6 8.1 %copy-start.28 = (s32[128]{0:T(128)S(1)}, s32[128]{0:T(128)}, u32[]{:S(2)}) copy-start(s32[128]{0:T(128)} %copy-done.26) | copy-start | bytes 1540
  538.6 8.1 %copy-start.39 = (s32[8]{0:T(128)S(1)}, s32[8]{0:T(128)}, u32[]{:S(2)}) copy-start(s32[8]{0:T(128)} %get-tuple-element.44) | copy-start | bytes 100
  541.7 80.8 %copy-start.12 = (bf16[128,1024]{1,0:T(8,128)(2,1)}, bf16[128,1024]{1,0:T(8,128)(2,1)S(1)}, u32[]{:S(2)}) copy-start(bf16[128,1024]{1,0:T(8,128)(2,1)S(1)} %get-tuple-element.10) | copy-start | bytes 786436
  (4 other events, 4.3 us)
Sparse Core Ops, SparseCore 0:
  10.2 43.3 all-gather.2
  55.7 37.1 all-gather.4
  114.3 20.3 reduce-scatter.2
  315.6 144.3 reduce-scatter.4
  622.6 17.3 all-reduce.1
where the time goes:
time: 714 us; the launch traced here: 713 us
  blocking collectives  303 us (42%)
  waiting for transfers between devices  247 us (35%)
  local copies, waits for them, and re-layouts  47.1 us (7%)
  matrix products  45.5 us (6%)
  other arithmetic  28.3 us (4%)
  starting transfers between devices  27.1 us (4%)
  between operations  14.6 us (2%)
    reduce_scatter x1, waiting for transfers between devices, on_device(): lax.psum_scatter(partial_out, 'tp', scatter_dimension=2, tiled=True)  144 us
    all_to_all x1, blocking collectives, on_device(): lax.all_to_all(outgoing, 'seq', split_axis=0, concat_axis=0, tiled=True)  143 us
    psum x1, blocking collectives, on_device(): chosen = lax.psum(chosen, 'seq').astype(bf16)  70.3 us
    all_to_all x1, waiting for transfers between devices, on_device(): lax.all_to_all(summed, 'seq', split_axis=0, concat_axis=0, tiled=True)  58.6 us
    pmax x1, blocking collectives, on_device(): peak_logit = lax.pmax(jnp.max(logits, -1), 'seq')  32.9 us
    psum x1, blocking collectives, on_device(): lax.psum(jnp.sum(jnp.exp(logits - peak_logit[:, None]), -1), 'seq')  29.5 us
    ppermute x4, starting transfers between devices, from_behind(): lax.ppermute(value, axis, [(source, source + steps) for source in range(l...  20.8 us
    psum x1, waiting for transfers between devices, on_device(): logits = lax.psum(jnp.dot(chosen, w_head, preferred_element_type=f32), 'tp')  17.5 us
  transfers between devices with their start and end apart: 10, of which 5 were waited for; matrix products, arithmetic and copies ran while one was open for 8% of the time, Pallas kernels for 0%

commit v1 on v0

--- a/solution.py
+++ b/solution.py
@@ -128,67 +128,83 @@
         local_index[None, :] <= local_index[:, None]
     )
     state = attend(state, query, key_rows, value_rows, own_allowed)
-    both_rows = jnp.stack([key_rows, value_rows])
-    moving = both_rows
+    both_rows = jnp.concatenate([key_rows, value_rows], 1)
+    behind = [from_behind(both_rows, "seq", step) for step in range(1, SPAN + 1)]
+    half = heads * HD
     for step in range(1, SPAN + 1):
-        moving = from_behind(moving, "seq", 1)
+        moving = behind[step - 1]
         key_index = (seq_index - step) * tok_dev + jnp.arange(tok_dev)
         key_request = request_of(key_index, ends)
         allowed = (key_index >= 0)[None, :] & (own_request[:, None] == key_request[None, :])
-        state = attend(state, query, moving[0], moving[1], allowed)
+        state = attend(state, query, moving[:, :half], moving[:, half:], allowed)
     best, total, accum = state
     attended = (accum / total[..., None]).astype(bf16)
     attended = jnp.transpose(attended, (1, 0, 2)).reshape(tok_dev, heads * HD)
-    mixed = jnp.dot(attended, w_out, preferred_element_type=f32)
-    attn_part = lax.psum_scatter(mixed, "tp", scatter_dimension=1, tiled=True)
-    resid = (tokens.astype(f32) + attn_part).astype(bf16)
-    resid_f = resid.astype(f32)
-    squares = lax.psum(jnp.sum(resid_f * resid_f, -1), "tp")
-    gain_part = lax.dynamic_slice_in_dim(moe_gain, tp_index * width_part, width_part, 0).astype(f32)
-    scaled = (resid_f * lax.rsqrt(squares / width + EPS)[:, None] * gain_part).astype(bf16)
-    moe_in = lax.all_gather(scaled, "tp", axis=1, tiled=True)
+    mixed = jnp.dot(attended, w_out, preferred_element_type=f32).astype(bf16)
+    parts = lax.all_gather(mixed, "tp", axis=0)
+    resid_full = (full_x.astype(f32) + jnp.sum(parts.astype(f32), 0)).astype(bf16)
+    moe_in = normalize(resid_full.astype(f32), moe_gain).astype(bf16)
+    resid = lax.dynamic_slice_in_dim(resid_full, tp_index * width_part, width_part, 1)
     experts = w_router.shape[1]
     topk = routes.shape[1]
     probs = jax.nn.softmax(jnp.dot(moe_in, w_router, preferred_element_type=f32), -1)
-    flat = routes.reshape(-1)
-    hits = (flat[:, None] == jnp.arange(experts)[None, :]).astype(jnp.int32)
-    rank = jnp.sum((jnp.cumsum(hits, 0) - hits) * hits, 1)
-    capacity = min(tok_dev, tp_count * max(1, 3 * tok_dev * topk // (2 * experts * tp_count)))
-    target = flat * capacity + rank
-    route_weight = jnp.sum(hits.reshape(tok_dev, topk, experts).astype(f32) * probs[:, None, :], -1)
-    repeated = jnp.repeat(moe_in, topk, axis=0)
-    outgoing = (
-        jnp.zeros((experts * capacity, width), bf16)
-        .at[target]
-        .set(repeated)
-        .reshape(experts, capacity, width)
-    )
-    arrived = lax.all_to_all(outgoing, "seq", split_axis=0, concat_axis=0, tiled=True)
-    sources = arrived.shape[0]
-    count = arrived.shape[1]
-    rows = arrived.reshape(sources * count, width)
-    gate = jnp.dot(rows, w_gate[0], preferred_element_type=f32)
-    up = jnp.dot(rows, w_up[0], preferred_element_type=f32)
-    act = (jax.nn.silu(gate) * up).astype(bf16)
-    partial_out = jnp.dot(act, w_down[0], preferred_element_type=f32).reshape(sources, count, width)
-    summed = lax.psum_scatter(partial_out, "tp", scatter_dimension=2, tiled=True).astype(bf16)
-    returned = lax.all_to_all(summed, "seq", split_axis=0, concat_axis=0, tiled=True)
-    picked = returned.reshape(experts * capacity, width_part)[target].reshape(
-        tok_dev, topk, width_part
-    )
-    moe_part = jnp.sum(picked.astype(f32) * route_weight[:, :, None], 1)
+    if 2 * topk >= experts:
+        named = routes[:, :, None] == jnp.arange(experts)[None, None, :]
+        share = jnp.sum(jnp.where(named, probs[:, None, :], 0.0), 1)
+        shares = lax.all_gather(share, "seq", axis=0, tiled=True)
+        own_share = lax.dynamic_slice_in_dim(shares, seq_index, 1, 1)
+        rows = lax.all_gather(moe_in, "seq", axis=0, tiled=True)
+        gate = jnp.dot(rows, w_gate[0], preferred_element_type=f32)
+        up = jnp.dot(rows, w_up[0], preferred_element_type=f32)
+        act = (jax.nn.silu(gate) * up).astype(bf16)
+        partial_out = (jnp.dot(act, w_down[0], preferred_element_type=f32) * own_share).astype(bf16)
+        summed = lax.psum_scatter(partial_out, "seq", scatter_dimension=0, tiled=True)
+        moe_part = lax.psum_scatter(summed, "tp", scatter_dimension=1, tiled=True).astype(f32)
+    else:
+        flat = routes.reshape(-1)
+        hits = (flat[:, None] == jnp.arange(experts)[None, :]).astype(jnp.int32)
+        rank = jnp.sum((jnp.cumsum(hits, 0) - hits) * hits, 1)
+        capacity = min(tok_dev, tp_count * max(1, 3 * tok_dev * topk // (2 * experts * tp_count)))
+        target = flat * capacity + rank
+        route_weight = jnp.sum(hits.reshape(tok_dev, topk, experts).astype(f32) * probs[:, None, :], -1)
+        repeated = jnp.repeat(moe_in, topk, axis=0)
+        outgoing = (
+            jnp.zeros((experts * capacity, width), bf16)
+            .at[target]
+            .set(repeated)
+            .reshape(experts, capacity, width)
+        )
+        arrived = lax.all_to_all(outgoing, "seq", split_axis=0, concat_axis=0, tiled=True)
+        sources = arrived.shape[0]
+        count = arrived.shape[1]
+        rows = arrived.reshape(sources * count, width)
+        gate = jnp.dot(rows, w_gate[0], preferred_element_type=f32)
+        up = jnp.dot(rows, w_up[0], preferred_element_type=f32)
+        act = (jax.nn.silu(gate) * up).astype(bf16)
+        partial_out = jnp.dot(act, w_down[0], preferred_element_type=f32).reshape(sources, count, width)
+        summed = lax.psum_scatter(partial_out, "tp", scatter_dimension=2, tiled=True).astype(bf16)
+        returned = lax.all_to_all(summed, "seq", split_axis=0, concat_axis=0, tiled=True)
+        picked = returned.reshape(experts * capacity, width_part)[target].reshape(
+            tok_dev, topk, width_part
+        )
+        moe_part = jnp.sum(picked.astype(f32) * route_weight[:, :, None], 1)
     hidden = (resid.astype(f32) + moe_part).astype(bf16)
-    hidden_f = hidden.astype(f32)
-    final_sq = lax.psum(jnp.sum(hidden_f * hidden_f, -1), "tp")
-    final = (hidden_f * lax.rsqrt(final_sq / width + EPS)[:, None] * final_gain.astype(f32)).astype(
+    last_hit = ((ends - 1)[:, None] == local_index[None, :]).astype(bf16)
+    chosen = jnp.dot(last_hit, hidden, preferred_element_type=f32)
+    lane_tp = jnp.arange(tp_count)[None, :, None]
+    spread = jnp.where(lane_tp == tp_index, chosen[:, None, :], 0.0).reshape(chosen.shape[0], width)
+    last = lax.psum(spread, ("seq", "tp"))
+    final_sq = jnp.sum(last * last, -1)
+    own_last = lax.dynamic_slice_in_dim(last, tp_index * width_part, width_part, 1)
+    final = (own_last * lax.rsqrt(final_sq / width + EPS)[:, None] * final_gain.astype(f32)).astype(
         bf16
     )
-    last_hit = ((ends - 1)[:, None] == local_index[None, :]).astype(bf16)
-    chosen = jnp.dot(last_hit, final, preferred_element_type=f32)
-    chosen = lax.psum(chosen, "seq").astype(bf16)
-    logits = lax.psum(jnp.dot(chosen, w_head, preferred_element_type=f32), "tp")
-    peak_logit = lax.pmax(jnp.max(logits, -1), "seq")
-    total_exp = lax.psum(jnp.sum(jnp.exp(logits - peak_logit[:, None]), -1), "seq")
+    logits = lax.psum(jnp.dot(final, w_head, preferred_element_type=f32), "tp")
+    peak_own = jnp.max(logits, -1)
+    total_own = jnp.sum(jnp.exp(logits - peak_own[:, None]), -1)
+    pairs = lax.all_gather(jnp.stack([peak_own, total_own]), "seq", axis=0)
+    peak_logit = jnp.max(pairs[:, 0], 0)
+    total_exp = jnp.sum(pairs[:, 1] * jnp.exp(pairs[:, 0] - peak_logit[None, :]), 0)
     log_probs = logits - peak_logit[:, None] - jnp.log(total_exp)[:, None]
     return (hidden, log_probs)
 

time: 714 us -> 549 us (0.77)
  blocking collectives: 303 us -> 54 us
  waiting for transfers between devices: 247 us -> 365 us
  local copies, waits for them, and re-layouts: 47.1 us -> 25.3 us
  starting transfers between devices: 27.1 us -> 14.7 us
  other arithmetic: 28.3 us -> 17.6 us
  matrix products: 45.5 us -> 55.9 us
    all_to_all x1 -> x0, blocking collectives: 143 us -> none  [on_device(): lax.all_to_all(outgoing, 'seq', split_axis=0, concat_axis=0, tiled=True)]
    psum x1 -> x2, waiting for transfers between devices: 17.5 us -> 145 us  [the longest x1 123 us: on_device(): last = lax.psum(spread, ('seq', 'tp'))]
    psum x4 -> x0, blocking collectives: 110 us -> none  [the longest x1 70.3 us: on_device(): chosen = lax.psum(chosen, 'seq').astype(bf16)]
    all_gather x0 -> x2, waiting for transfers between devices: none -> 95.4 us  [the longest x1 51.5 us: on_device(): rows = lax.all_gather(moe_in, 'seq', axis=0, tiled=True)]
    all_to_all x1 -> x0, waiting for transfers between devices: 58.6 us -> none  [on_device(): lax.all_to_all(summed, 'seq', split_axis=0, concat_axis=0, tiled=True)]
    reduce_scatter x2, waiting for transfers between devices: 159 us -> 119 us  [the longest x1 103 us: on_device(): lax.psum_scatter(partial_out, 'seq', scatter_dimension=0, tiled=True)]
    all_gather x1 -> x2, blocking collectives: 7.52 us -> 43.8 us  [the longest x1 22.4 us: on_device(): shares = lax.all_gather(share, 'seq', axis=0, tiled=True)]
    pmax x1 -> x0, blocking collectives: 32.9 us -> none  [on_device(): peak_logit = lax.pmax(jnp.max(logits, -1), 'seq')]
  transfers between devices with their start and end apart: 10 -> 12, of which waited for: 5 -> 7; matrix products, arithmetic and copies ran while one was open for 8% -> 10% of each run, Pallas kernels for 0% -> 0%
where the time goes in v1:
time: 549 us; the launch traced here: 548 us
  waiting for transfers between devices  365 us (66%)
  matrix products  55.9 us (10%)
  blocking collectives  54 us (10%)
  local copies, waits for them, and re-layouts  25.3 us (5%)
  other arithmetic  17.6 us (3%)
  between operations  15.2 us (3%)
  starting transfers between devices  14.7 us (3%)
    psum x1, waiting for transfers between devices, on_device(): last = lax.psum(spread, ('seq', 'tp'))  123 us
    reduce_scatter x1, waiting for transfers between devices, on_device(): lax.psum_scatter(partial_out, 'seq', scatter_dimension=0, tiled=True)  103 us
    all_gather x1, waiting for transfers between devices, on_device(): rows = lax.all_gather(moe_in, 'seq', axis=0, tiled=True)  51.5 us
    all_gather x1, waiting for transfers between devices, on_device(): parts = lax.all_gather(mixed, 'tp', axis=0)  43.9 us
    all_gather x1, blocking collectives, on_device(): shares = lax.all_gather(share, 'seq', axis=0, tiled=True)  22.4 us
    psum x1, waiting for transfers between devices, on_device(): logits = lax.psum(jnp.dot(final, w_head, preferred_element_type=f32), 'tp')  21.9 us
    all_gather x1, blocking collectives, on_device(): pairs = lax.all_gather(jnp.stack([peak_own, total_own]), 'seq', axis=0)  21.3 us
    reduce_scatter x1, waiting for transfers between devices, on_device(): lax.psum_scatter(summed, 'tp', scatter_dimension=1, tiled=True).astype(f32)  16.3 us
  transfers between devices with their start and end apart: 12, of which 7 were waited for; matrix products, arithmetic and copies ran while one was open for 10% of the time, Pallas kernels for 0%

profile of v1, /device:TPU:0, one launch (start us, length us, event | category | flops | bytes accessed | tf_op | source)
XLA Modules:
  0.0 547.7 jit_solution(15677610911807309942)
XLA Ops:
  8.0 10.2 %all_gather.27 = bf16[128,2048]{1,0:T(8,128)(2,1)S(1)} all-gather(bf16[128,1024]{1,0:T(8,128)(2,1)} %param.19), channel_id=1, replica_groups=mesh['seq'=16,'tp'=2] {'tp'}, dimensions={1}, use_global_device_ids=true | all-gather | bytes 786432 | tf_op jit(solution)/shard_map/all_gather | solution.py:94
  19.1 4.0 fusion.111
  23.9 1.1 copy.138
  25.0 1.0 copy.139
  28.5 1.2 multiply_subtract_fusion
  30.9 3.0 convolution_convert_fusion.1
  34.7 2.1 collective-permute-start
  36.8 4.2 collective-permute-start.1
  41.0 4.4 collective-permute-start.2
  45.4 3.5 collective-permute-start.3
  49.2 2.9 convolution_bitcast_fusion.6
  55.2 1.8 fusion.119
  57.9 5.0 collective-permute-done.2
  62.9 1.8 fusion.120
  64.7 1.8 copy.134
  66.6 1.9 slice_bitcast_fusion
  68.4 1.8 copy.135
  70.2 1.9 fusion.118
  72.1 1.8 copy.132
  73.9 2.7 fusion.126
  76.6 2.6 fusion.125
  79.2 1.7 fusion.124
  80.9 1.7 fusion.123
  82.6 2.3 copy.100
  85.0 1.9 fusion.4
  90.0 1.1 convolution_bitcast_fusion.2
  92.2 2.3 copy.111
  94.6 2.7 fusion.23
  98.1 1.5 copy-done.2
  99.5 1.6 convolution_convert_fusion
  101.2 43.9 %all-gather.14.cloned.1.call-done = bf16[256,2048]{1,0:T(8,128)(2,1)} async-done(((bf16[128,2048]{1,0:T(8,128)(2,1)}), bf16[256,2048]{1,0:T(8,128)(2,1)}) %all-gather.14.cloned.1.call-update) | async-done | bytes 1048592 | tf_op jit(solution)/shard_map/all_gather | solution.py:144
  145.2 1.5 convert_reduce_fusion
  147.0 1.0 fusion.27
  148.1 1.3 fusion.128
  149.5 22.4 %all_gather.33 = f32[2048,16]{0,1:T(8,128)S(1)} all-gather(f32[128,16]{0,1:T(8,128)S(1)} %select_reduce_fusion), channel_id=1, replica_groups=mesh['seq'=16,'tp'=2] {'seq'}, dimensions={0}, use_global_device_ids=true | all-gather | bytes 139264 | tf_op jit(solution)/shard_map/all_gather | solution.py:154
  171.9 51.5 %all-gather.12.cloned.1.call-done = bf16[2048,2048]{1,0:T(8,128)(2,1)} async-done(((bf16[128,2048]{1,0:T(8,128)(2,1)}), bf16[2048,2048]{1,0:T(8,128)(2,1)}) %all-gather.12.cloned.1.call-update) | async-done | bytes 8388624 | tf_op jit(solution)/shard_map/all_gather | solution.py:156
  223.4 7.7 %fusion.2 = f32[2048,512]{1,0:T(8,128)S(1)} fusion(bf16[2048,2048]{1,0:T(8,128)(2,1)} %all-gather.12.cloned.1.call-done, bf16[1,2048,512]{2,1,0:T(8,128)(2,1)} %param.32), kind=kOutput, calls=%fused_computation.6 | convolution fusion | flops 4294967296 | bytes 14680064 | tf_op jit(solution)/shard_map/dot_general | solution.py:157
  231.1 5.2 multiply_convert_fusion.1
  236.3 6.7 %multiply_convert_fusion = bf16[2048,2048]{1,0:T(8,128)(2,1)} fusion(bf16[2048,512]{1,0:T(8,128)(2,1)S(1)} %multiply_convert_fusion.1, f32[2048]{0:T(1024)S(1)} %bitcast.237, bf16[1,512,2048]{2,1,0:T(8,128)(2,1)S(1)} %copy-done), kind=kOutput, calls=%fused_computation | convolution fusion | flops 4303355904 | bytes 12591104 | tf_op jit(solution)/shard_map/dot_general | solution.py:160
  243.1 102.9 %reduce-scatter.3.cloned.1.call-done = bf16[128,2048]{1,0:T(8,128)(2,1)} async-done(((bf16[2048,2048]{1,0:T(8,128)(2,1)}), bf16[128,2048]{1,0:T(8,128)(2,1)}) %reduce-scatter.3.cloned.1.call-update) | async-done | bytes 524304 | tf_op jit(solution)/shard_map/reduce_scatter | solution.py:161
  346.3 16.3 %reduce-scatter.5.cloned.1.call-done = bf16[128,1024]{1,0:T(8,128)(2,1)} async-done(((bf16[128,2048]{1,0:T(8,128)(2,1)}), bf16[128,1024]{1,0:T(8,128)(2,1)}) %reduce-scatter.5.cloned.1.call-update) | async-done | bytes 262160 | tf_op jit(solution)/shard_map/reduce_scatter | solution.py:162
  364.5 122.6 %all-reduce.3.cloned.1.call-done = f32[8,2048]{1,0:T(8,128)} async-done(((f32[8,2048]{1,0:T(8,128)}), f32[8,2048]{1,0:T(8,128)}) %all-reduce.3.cloned.1.call-update) | async-done | bytes 65552 | tf_op jit(solution)/shard_map/psum | solution.py:196
  488.2 5.3 fusion.76
  493.5 21.9 %all-reduce.5.cloned.1.call-done = f32[8,3144]{1,0:T(8,128)} async-done(((f32[8,3144]{1,0:T(8,128)}), f32[8,3144]{1,0:T(8,128)}) %all-reduce.5.cloned.1.call-update) | async-done | bytes 100624 | tf_op jit(solution)/shard_map/psum | solution.py:202
  515.4 1.0 reduce_max.103
  516.4 1.1 exponential_reduce_fusion
  517.5 21.3 %all-gather.2 = f32[16,2,8]{2,1,0:T(2,128)S(1)} all-gather(f32[1,2,8]{2,1,0:T(2,128)S(1)} %maximum_bitcast_fusion), channel_id=3, replica_groups=mesh['seq'=16,'tp'=2] {'seq'}, dimensions={0}, use_global_device_ids=true | all-gather | bytes 1088 | tf_op jit(solution)/shard_map/all_gather | solution.py:205
  539.2 1.6 subtract_subtract_fusion
  (210 shorter events, 19.5 us)
Async XLA Ops:
  7.2 229.1 %copy-start = (bf16[1,512,2048]{2,1,0:T(8,128)(2,1)S(1)}, bf16[1,512,2048]{2,1,0:T(8,128)(2,1)}, u32[]{:S(2)}) copy-start(bf16[1,512,2048]{2,1,0:T(8,128)(2,1)} %param.34) | copy-start | bytes 6291460
  7.2 75.4 %all-gather.8.cloned.1.call-start = ((), (), s32[]{:S(2)}) async-start(), calls=%async_computation.2 | async-start | bytes 1114112 | tf_op jit(solution)/shard_map/all_gather | solution.py:119
  7.9 84.2 %all-gather.10.cloned.1.call-start = ((), (), s32[]{:S(2)}) async-start(), calls=%async_computation.3 | async-start | bytes 1114112 | tf_op jit(solution)/shard_map/all_gather | solution.py:120
  23.1 3.0 copy-start.59
  23.1 4.4 copy-start.57
  26.3 3.7 copy-start.37
  26.9 3.1 copy-start.40
  29.8 4.1 copy-start.3
  30.9 3.0 copy-start.15
  34.7 35.5 %collective-permute-start = (bf16[128,2048]{1,0:T(8,128)(2,1)}, bf16[128,2048]{1,0:T(8,128)(2,1)}, u32[]{:S(2)}, u32[]{:S(2)}) collective-permute-start(bf16[128,2048]{1,0:T(8,128)(2,1)} %pad_maximum_fusion), channel_id=1, source_target_pairs={{0,2},{2,4},{4,6},{6,8},{8,10},{10,12},{12,14},{14,16},{16,18},{18... | collective-permute-start | bytes 1572872 | tf_op jit(solution)/shard_map/ppermute | solution.py:17
  36.8 18.4 %collective-permute-start.1 = (bf16[128,2048]{1,0:T(8,128)(2,1)}, bf16[128,2048]{1,0:T(8,128)(2,1)}, u32[]{:S(2)}, u32[]{:S(2)}) collective-permute-start(bf16[128,2048]{1,0:T(8,128)(2,1)} %pad_maximum_fusion), channel_id=1, source_target_pairs={{0,4},{2,6},{4,8},{6,10},{8,12},{10,14},{12,16},{14,18},{16,20},{1... | collective-permute-start | bytes 1572872 | tf_op jit(solution)/shard_map/ppermute | solution.py:17
  41.0 21.9 %collective-permute-start.2 = (bf16[128,2048]{1,0:T(8,128)(2,1)}, bf16[128,2048]{1,0:T(8,128)(2,1)}, u32[]{:S(2)}, u32[]{:S(2)}) collective-permute-start(bf16[128,2048]{1,0:T(8,128)(2,1)} %pad_maximum_fusion), channel_id=1, source_target_pairs={{0,6},{2,8},{4,10},{6,12},{8,14},{10,16},{12,18},{14,20},{16,22},{... | collective-permute-start | bytes 1572872 | tf_op jit(solution)/shard_map/ppermute | solution.py:17
  45.4 21.2 %collective-permute-start.3 = (bf16[128,2048]{1,0:T(8,128)(2,1)}, bf16[128,2048]{1,0:T(8,128)(2,1)}, u32[]{:S(2)}, u32[]{:S(2)}) collective-permute-start(bf16[128,2048]{1,0:T(8,128)(2,1)} %pad_maximum_fusion), channel_id=1, source_target_pairs={{0,8},{2,10},{4,12},{6,14},{8,16},{10,18},{12,20},{14,22},{16,24},... | collective-permute-start | bytes 1572872 | tf_op jit(solution)/shard_map/ppermute | solution.py:17
  48.9 96.2 %all-gather.14.cloned.1.call-start = ((), (), s32[]{:S(2)}) async-start(), calls=%async_computation.9 | async-start | bytes 1572864 | tf_op jit(solution)/shard_map/all_gather | solution.py:144
  64.7 9.2 %copy-start.6 = (bf16[128,8,128]{2,0,1:T(8,128)(2,1)S(1)}, bf16[128,8,128]{2,0,1:T(8,128)(2,1)}, u32[]{:S(2)}) copy-start(bf16[128,8,128]{2,0,1:T(8,128)(2,1)} %copy-done.5) | copy-start | bytes 786436
  73.9 5.3 copy-start.22
  73.9 7.0 %copy-start.23 = (bf16[16,8,8,128]{3,2,1,0:T(8,128)(2,1)S(1)}, bf16[16,8,8,128]{3,2,1,0:T(8,128)(2,1)}, u32[]{:S(2)}) copy-start(bf16[16,8,8,128]{3,2,1,0:T(8,128)(2,1)} %get-tuple-element.31) | copy-start | bytes 786436
  85.0 2.6 copy-start.9
  87.5 2.5 copy-start.12
  87.6 3.5 copy-start.13
  90.0 4.4 copy-start.31
  91.1 3.3 copy-start.48
  91.1 3.3 copy-start.49
  94.4 2.9 copy-start.10
  94.4 2.9 copy-start.26
  94.5 2.9 copy-start.32
  94.5 3.1 copy-start.17
  94.5 3.1 copy-start.18
  94.5 3.1 copy-start.19
  94.5 3.1 copy-start.20
  94.5 3.1 copy-start.21
  94.5 3.1 copy-start.29
  94.5 3.1 copy-start.44
  94.5 3.1 copy-start.45
  94.5 3.1 copy-start.46
  94.6 3.1 copy-start.47
  101.1 122.3 %all-gather.12.cloned.1.call-start = ((), (), s32[]{:S(2)}) async-start(), calls=%async_computation.4 | async-start | bytes 8912896 | tf_op jit(solution)/shard_map/all_gather | solution.py:156
  146.7 2.7 copy-start.43
  148.0 198.1 %reduce-scatter.3.cloned.1.call-start = ((), (), s32[]{:S(2)}) async-start(), calls=%async_computation.5 | async-start | bytes 8912896 | tf_op jit(solution)/shard_map/reduce_scatter | solution.py:161
  223.4 7.7 %copy-start.60 = (bf16[2048,2048]{1,0:T(8,128)(2,1)S(1)}, bf16[2048,2048]{1,0:T(8,128)(2,1)}, u32[]{:S(2)}) copy-start(bf16[2048,2048]{1,0:T(8,128)(2,1)} %all-gather.12.cloned.1.call-done) | copy-start | bytes 25165828
  223.4 7.7 %copy-start.61 = (bf16[1,2048,512]{2,1,0:T(8,128)(2,1)S(1)}, bf16[1,2048,512]{2,1,0:T(8,128)(2,1)}, u32[]{:S(2)}) copy-start(bf16[1,2048,512]{2,1,0:T(8,128)(2,1)} %param.33) | copy-start | bytes 6291460
  243.1 120.5 %copy-start.39 = (s32[128]{0:T(128)S(1)}, s32[128]{0:T(128)}, u32[]{:S(2)}) copy-start(s32[128]{0:T(128)} %copy-done.37) | copy-start | bytes 1540
  243.1 120.5 %copy-start.51 = (s32[8]{0:T(128)S(1)}, s32[8]{0:T(128)}, u32[]{:S(2)}) copy-start(s32[8]{0:T(128)} %get-tuple-element.45) | copy-start | bytes 100
  243.1 121.5 %copy-start.56 = (bf16[1024]{0:T(1024)(128)(2,1)S(1)}, bf16[1024]{0:T(1024)(128)(2,1)}, u32[]{:S(2)}) copy-start(bf16[1024]{0:T(1024)(128)(2,1)} %param.36) | copy-start | bytes 6148
  243.1 119.5 %reduce-scatter.5.cloned.1.call-start = ((), (), s32[]{:S(2)}) async-start(), calls=%async_computation.6 | async-start | bytes 786432 | tf_op jit(solution)/shard_map/reduce_scatter | solution.py:162
  346.1 141.1 %all-reduce.3.cloned.1.call-start = ((), (), s32[]{:S(2)}) async-start(), calls=%async_computation.7 | async-start | bytes 131072 | tf_op jit(solution)/shard_map/psum | solution.py:196
  363.6 129.9 %copy-start.14 = (bf16[128,1024]{1,0:T(8,128)(2,1)}, bf16[128,1024]{1,0:T(8,128)(2,1)S(1)}, u32[]{:S(2)}) copy-start(bf16[128,1024]{1,0:T(8,128)(2,1)S(1)} %add_convert_fusion) | copy-start | bytes 786436
  364.5 150.9 %all-reduce.5.cloned.1.call-start = ((), (), s32[]{:S(2)}) async-start(), calls=%async_computation.8 | async-start | bytes 204800 | tf_op jit(solution)/shard_map/psum | solution.py:202
  (26 other events, 39.4 us)
Sparse Core Ops, SparseCore 0:
  10.2 41.4 all-gather.7
  53.9 37.1 all-gather.9
  101.3 43.8 all-gather.13
  148.1 75.2 all-gather.11
  243.2 102.8 reduce-scatter.2
  348.2 14.3 reduce-scatter.4
  369.6 117.5 all-reduce.2
  493.6 21.7 all-reduce.4

commit v2 on v1

--- a/solution.py
+++ b/solution.py
@@ -1,10 +1,13 @@
 import jax
 import jax.numpy as jnp
 from jax import lax
+from jax.experimental import pallas as pl
+from jax.experimental.pallas import tpu as pltpu
 from jax.sharding import PartitionSpec as P
 
 HD = 128
 SPAN = 4
+VMEM = pltpu.VMEM
 
 
 EPS = 1e-05
@@ -58,6 +61,180 @@
         "htk,khd->htd", weights.astype(jnp.bfloat16), values, preferred_element_type=jnp.float32
     )
     return (top, total, accum)
+
+
+def partner(axis, bit):
+    index = lax.axis_index(axis)
+    span = 1 << bit
+    other = index + span - 2 * span * ((index // span) % 2)
+    return {axis: other}
+
+
+def greet(stages):
+    barrier = pltpu.get_barrier_semaphore()
+    for axis, bit in stages:
+        pl.semaphore_signal(barrier, inc=1, device_id=partner(axis, bit))
+    pl.semaphore_wait(barrier, len(stages))
+
+
+def swap(source, target, send_sem, recv_sem, stage):
+    copy = pltpu.make_async_remote_copy(
+        src_ref=source, dst_ref=target, send_sem=send_sem, recv_sem=recv_sem,
+        device_id=partner(*stage),
+    )
+    copy.start()
+    return copy
+
+
+def bits_of(axis):
+    return [(axis, bit) for bit in range(lax.axis_size(axis).bit_length() - 1)]
+
+
+def last_rows(chosen, gain, width):
+    seq_stages, tp_stages = bits_of("seq"), bits_of("tp")
+    stages = seq_stages + tp_stages
+    rows, part = chosen.shape
+
+    def kernel(chosen_ref, gain_ref, out_ref, held, got, sq_held, sq_got, send_sem, recv_sem):
+        greet(stages)
+        held[0] = chosen_ref[...]
+        count = len(seq_stages)
+        for k, stage in enumerate(seq_stages):
+            swap(held.at[k], got.at[k], send_sem.at[k], recv_sem.at[k], stage).wait()
+            held[k + 1] = held[k] + got[k]
+        total = held[count]
+        sq_held[0] = jnp.broadcast_to(jnp.sum(total * total, -1, keepdims=True), (rows, 128))
+        for k, stage in enumerate(tp_stages):
+            n = count + k
+            swap(sq_held.at[k], sq_got.at[k], send_sem.at[n], recv_sem.at[n], stage).wait()
+            sq_held[k + 1] = sq_held[k] + sq_got[k]
+        square = sq_held[len(tp_stages)][:, :1]
+        scaled = total * lax.rsqrt(square / width + EPS) * gain_ref[...].astype(jnp.float32)
+        out_ref[...] = scaled.astype(jnp.bfloat16)
+
+    ns, nt = len(seq_stages), len(tp_stages)
+    return pl.pallas_call(
+        kernel,
+        out_shape=jax.ShapeDtypeStruct((rows, part), jnp.bfloat16),
+        in_specs=[pl.BlockSpec(memory_space=VMEM)] * 2,
+        out_specs=pl.BlockSpec(memory_space=VMEM),
+        scratch_shapes=[
+            VMEM((ns + 1, rows, part), jnp.float32),
+            VMEM((ns, rows, part), jnp.float32),
+            VMEM((nt + 1, rows, 128), jnp.float32),
+            VMEM((nt, rows, 128), jnp.float32),
+            pltpu.SemaphoreType.DMA((ns + nt,)),
+            pltpu.SemaphoreType.DMA((ns + nt,)),
+        ],
+        compiler_params=pltpu.CompilerParams(collective_id=1, has_side_effects=True),
+        name="last_rows",
+    )(chosen, gain.reshape(1, part))
+
+
+def log_softmax(logits):
+    seq_stages, tp_stages = bits_of("seq"), bits_of("tp")
+    stages = tp_stages + seq_stages
+    rows, part = logits.shape
+
+    def kernel(logits_ref, out_ref, held, got, st_held, st_got, send_sem, recv_sem):
+        greet(stages)
+        held[0] = logits_ref[...]
+        count = len(tp_stages)
+        for k, stage in enumerate(tp_stages):
+            swap(held.at[k], got.at[k], send_sem.at[k], recv_sem.at[k], stage).wait()
+            held[k + 1] = held[k] + got[k]
+        total = held[count]
+        peak = jnp.max(total, -1, keepdims=True)
+        mass = jnp.sum(jnp.exp(total - peak), -1, keepdims=True)
+        st_held[0, :, :128] = jnp.broadcast_to(peak, (rows, 128))
+        st_held[0, :, 128:] = jnp.broadcast_to(mass, (rows, 128))
+        for k, stage in enumerate(seq_stages):
+            n = count + k
+            swap(st_held.at[k], st_got.at[k], send_sem.at[n], recv_sem.at[n], stage).wait()
+            mine, theirs = st_held[k, :, :128], st_got[k, :, :128]
+            top = jnp.maximum(mine, theirs)
+            st_held[k + 1, :, :128] = top
+            st_held[k + 1, :, 128:] = st_held[k, :, 128:] * jnp.exp(mine - top) + st_got[
+                k, :, 128:
+            ] * jnp.exp(theirs - top)
+        last = len(seq_stages)
+        out_ref[...] = total - st_held[last, :, :1] - jnp.log(st_held[last, :, 128:129])
+
+    ns, nt = len(seq_stages), len(tp_stages)
+    return pl.pallas_call(
+        kernel,
+        out_shape=jax.ShapeDtypeStruct((rows, part), jnp.float32),
+        in_specs=[pl.BlockSpec(memory_space=VMEM)],
+        out_specs=pl.BlockSpec(memory_space=VMEM),
+        scratch_shapes=[
+            VMEM((nt + 1, rows, part), jnp.float32),
+            VMEM((nt, rows, part), jnp.float32),
+            VMEM((ns + 1, rows, 256), jnp.float32),
+            VMEM((ns, rows, 256), jnp.float32),
+            pltpu.SemaphoreType.DMA((ns + nt,)),
+            pltpu.SemaphoreType.DMA((ns + nt,)),
+        ],
+        compiler_params=pltpu.CompilerParams(collective_id=2, has_side_effects=True),
+        name="log_softmax",
+    )(logits)
+
+
+def gather_columns(block):
+    stages = bits_of("tp")
+    rows, part = block.shape
+    count = lax.axis_size("tp")
+
+    def kernel(block_ref, out_ref, send_sem, recv_sem):
+        greet(stages)
+        me = lax.axis_index("tp")
+        out_ref[:, pl.ds(pl.multiple_of(me * part, part), part)] = block_ref[...]
+        for k, stage in enumerate(stages):
+            wide = part << k
+            start = pl.multiple_of((me // (1 << k)) * wide, wide)
+            piece = out_ref.at[:, pl.ds(start, wide)]
+            swap(piece, piece, send_sem.at[k], recv_sem.at[k], stage).wait()
+
+    return pl.pallas_call(
+        kernel,
+        out_shape=jax.ShapeDtypeStruct((rows, part * count), block.dtype),
+        in_specs=[pl.BlockSpec(memory_space=VMEM)],
+        out_specs=pl.BlockSpec(memory_space=VMEM),
+        scratch_shapes=[pltpu.SemaphoreType.DMA((len(stages),))] * 2,
+        compiler_params=pltpu.CompilerParams(collective_id=3, has_side_effects=True),
+        name="gather_columns",
+    )(block)
+
+
+def sum_over_tp(block):
+    stages = bits_of("tp")
+    rows, part = block.shape
+
+    def kernel(block_ref, out_ref, held, got, send_sem, recv_sem):
+        greet(stages)
+        for k, stage in enumerate(stages):
+            source = block_ref if k == 0 else held.at[k]
+            swap(source, got.at[k], send_sem.at[k], recv_sem.at[k], stage).wait()
+            total = source[...].astype(jnp.float32) + got[k].astype(jnp.float32)
+            if k + 1 < len(stages):
+                held[k + 1] = total.astype(jnp.bfloat16)
+            else:
+                out_ref[...] = total
+
+    count = len(stages)
+    return pl.pallas_call(
+        kernel,
+        out_shape=jax.ShapeDtypeStruct((rows, part), jnp.float32),
+        in_specs=[pl.BlockSpec(memory_space=VMEM)],
+        out_specs=pl.BlockSpec(memory_space=VMEM),
+        scratch_shapes=[
+            VMEM((count, rows, part), jnp.bfloat16),
+            VMEM((count, rows, part), jnp.bfloat16),
+            pltpu.SemaphoreType.DMA((count,)),
+            pltpu.SemaphoreType.DMA((count,)),
+        ],
+        compiler_params=pltpu.CompilerParams(collective_id=4, has_side_effects=True),
+        name="sum_over_tp",
+    )(block)
 
 
 def on_device(
@@ -91,7 +268,7 @@
     width_part = tokens.shape[1]
     shard_rows = prefix_keys.shape[0]
     prefix_length = shard_rows * seq_count // 2
-    full_x = lax.all_gather(tokens, "tp", axis=1, tiled=True)
+    full_x = gather_columns(tokens)
     width = full_x.shape[1]
     normed = normalize(full_x.astype(f32), attn_gain).astype(bf16)
     heads = w_query.shape[1] // HD
@@ -141,8 +318,7 @@
     attended = (accum / total[..., None]).astype(bf16)
     attended = jnp.transpose(attended, (1, 0, 2)).reshape(tok_dev, heads * HD)
     mixed = jnp.dot(attended, w_out, preferred_element_type=f32).astype(bf16)
-    parts = lax.all_gather(mixed, "tp", axis=0)
-    resid_full = (full_x.astype(f32) + jnp.sum(parts.astype(f32), 0)).astype(bf16)
+    resid_full = (full_x.astype(f32) + sum_over_tp(mixed)).astype(bf16)
     moe_in = normalize(resid_full.astype(f32), moe_gain).astype(bf16)
     resid = lax.dynamic_slice_in_dim(resid_full, tp_index * width_part, width_part, 1)
     experts = w_router.shape[1]
@@ -191,21 +367,8 @@
     hidden = (resid.astype(f32) + moe_part).astype(bf16)
     last_hit = ((ends - 1)[:, None] == local_index[None, :]).astype(bf16)
     chosen = jnp.dot(last_hit, hidden, preferred_element_type=f32)
-    lane_tp = jnp.arange(tp_count)[None, :, None]
-    spread = jnp.where(lane_tp == tp_index, chosen[:, None, :], 0.0).reshape(chosen.shape[0], width)
-    last = lax.psum(spread, ("seq", "tp"))
-    final_sq = jnp.sum(last * last, -1)
-    own_last = lax.dynamic_slice_in_dim(last, tp_index * width_part, width_part, 1)
-    final = (own_last * lax.rsqrt(final_sq / width + EPS)[:, None] * final_gain.astype(f32)).astype(
-        bf16
-    )
-    logits = lax.psum(jnp.dot(final, w_head, preferred_element_type=f32), "tp")
-    peak_own = jnp.max(logits, -1)
-    total_own = jnp.sum(jnp.exp(logits - peak_own[:, None]), -1)
-    pairs = lax.all_gather(jnp.stack([peak_own, total_own]), "seq", axis=0)
-    peak_logit = jnp.max(pairs[:, 0], 0)
-    total_exp = jnp.sum(pairs[:, 1] * jnp.exp(pairs[:, 0] - peak_logit[None, :]), 0)
-    log_probs = logits - peak_logit[:, None] - jnp.log(total_exp)[:, None]
+    final = last_rows(chosen, final_gain, width)
+    log_probs = log_softmax(jnp.dot(final, w_head, preferred_element_type=f32))
     return (hidden, log_probs)
 
 

time: 549 us -> 403 us (0.73)
  waiting for transfers between devices: 365 us -> 179 us
  Pallas kernels: 0 us -> 59.8 us
  blocking collectives: 54 us -> 36.4 us
    psum x2 -> x0, waiting for transfers between devices: 145 us -> none  [the longest x1 123 us: on_device(): last = lax.psum(spread, ('seq', 'tp'))]
    pallas_call x0 -> x4, Pallas kernels: none -> 59.8 us  [the longest x1 17.5 us: last_rows(): pl.pallas_call(kernel, out_shape=jax.ShapeDtypeStruct((rows, part), jnp.b...]
    all_gather x1 -> x0, waiting for transfers between devices: 43.9 us -> none  [on_device(): parts = lax.all_gather(mixed, 'tp', axis=0)]
    all_gather x2 -> x0, blocking collectives: 31.5 us -> none  [the longest x1 21.3 us: on_device(): pairs = lax.all_gather(jnp.stack([peak_own, total_own]), 'seq', axis=0)]
    all_gather x1, blocking collectives: 22.4 us -> 36.4 us  [on_device(): shares = lax.all_gather(share, 'seq', axis=0, tiled=True)]
  transfers between devices with their start and end apart: 12 -> 9, of which waited for: 7 -> 4; matrix products, arithmetic and copies ran while one was open for 10% -> 14% of each run, Pallas kernels for 0% -> 3%
where the time goes in v2:
time: 403 us; the launch traced here: 402 us
  waiting for transfers between devices  179 us (44%)
  Pallas kernels  59.8 us (15%)
  matrix products  56.6 us (14%)
  blocking collectives  36.4 us (9%)
  local copies, waits for them, and re-layouts  27.1 us (7%)
  between operations  14.8 us (4%)
  starting transfers between devices  14.6 us (4%)
  other arithmetic  14.1 us (3%)
    reduce_scatter x1, waiting for transfers between devices, on_device(): lax.psum_scatter(partial_out, 'seq', scatter_dimension=0, tiled=True)  103 us
    all_gather x1, waiting for transfers between devices, on_device(): rows = lax.all_gather(moe_in, 'seq', axis=0, tiled=True)  55.9 us
    all_gather x1, blocking collectives, on_device(): shares = lax.all_gather(share, 'seq', axis=0, tiled=True)  36.4 us
    pallas_call x1, Pallas kernels, last_rows(): pl.pallas_call(kernel, out_shape=jax.ShapeDtypeStruct((rows, part), jnp.b...  17.5 us
    reduce_scatter x1, waiting for transfers between devices, on_device(): lax.psum_scatter(summed, 'tp', scatter_dimension=1, tiled=True).astype(f32)  15.8 us
    pallas_call x1, Pallas kernels, sum_over_tp(): pl.pallas_call(kernel, out_shape=jax.ShapeDtypeStruct((rows, part), jnp.f...  15.7 us
    pallas_call x1, Pallas kernels, log_softmax(): pl.pallas_call(kernel, out_shape=jax.ShapeDtypeStruct((rows, part), jnp.f...  15.6 us
    ppermute x4, starting transfers between devices, from_behind(): lax.ppermute(value, axis, [(source, source + steps) for source in range(l...  14.2 us
  transfers between devices with their start and end apart: 9, of which 4 were waited for; matrix products, arithmetic and copies ran while one was open for 14% of the time, Pallas kernels for 3%

profile of v2, /device:TPU:0, one launch (start us, length us, event | category | flops | bytes accessed | tf_op | source)
XLA Modules:
  0.0 402.1 jit_solution(12791285911512172056)
XLA Ops:
  8.0 11.1 %gather_columns.1 = bf16[128,2048]{1,0:T(8,128)(2,1)} custom-call(bf16[128,1024]{1,0:T(8,128)(2,1)} %block_ref.1), custom_call_target="tpu_custom_call" | custom-call | tf_op jit(solution)/shard_map/gather_columns/pallas_call | solution.py:197
  19.1 1.2 fusion.29
  21.0 4.1 %fusion.104 = f32[128,1024]{0,1:T(8,128)S(1)} fusion(bf16[2048,1024]{1,0:T(8,128)(2,1)} %param.22, bf16[128,2048]{1,0:T(8,128)(2,1)} %gather_columns.1, f32[2048]{0:T(1024)S(1)} %convert_element_type.106, f32[128]{0:T(128)S(1)} %add_rsqrt_fusion.1), kind=kOutput, calls=%fused_computation.195 | convolution fusion | flops 537919488 | bytes 5251584 | tf_op jit(solution)/shard_map/dot_general | solution.py:286
  25.9 1.1 copy.130
  30.5 1.2 multiply_subtract_fusion
  32.9 3.0 convolution_convert_fusion.1
  36.8 2.1 collective-permute-start
  38.9 4.3 %collective-permute-start.1 = (bf16[128,2048]{1,0:T(8,128)(2,1)}, bf16[128,2048]{1,0:T(8,128)(2,1)}, u32[]{:S(2)}, u32[]{:S(2)}) collective-permute-start(bf16[128,2048]{1,0:T(8,128)(2,1)} %pad_maximum_fusion), channel_id=1, source_target_pairs={{0,4},{2,6},{4,8},{6,10},{8,12},{10,14},{12,16},{14,18},{16,20},{1... | collective-permute-start | bytes 1572872 | tf_op jit(solution)/shard_map/ppermute | solution.py:20
  43.1 4.4 %collective-permute-start.2 = (bf16[128,2048]{1,0:T(8,128)(2,1)}, bf16[128,2048]{1,0:T(8,128)(2,1)}, u32[]{:S(2)}, u32[]{:S(2)}) collective-permute-start(bf16[128,2048]{1,0:T(8,128)(2,1)} %pad_maximum_fusion), channel_id=1, source_target_pairs={{0,6},{2,8},{4,10},{6,12},{8,14},{10,16},{12,18},{14,20},{16,22},{... | collective-permute-start | bytes 1572872 | tf_op jit(solution)/shard_map/ppermute | solution.py:20
  47.5 3.5 collective-permute-start.3
  51.3 2.9 convolution_bitcast_fusion.6
  57.3 1.3 convert_element_type.128
  58.6 1.8 fusion.112
  61.2 3.2 collective-permute-done.2
  64.4 1.8 fusion.113
  66.2 1.8 copy.126
  68.1 1.8 slice_bitcast_fusion
  69.9 1.8 copy.127
  71.7 1.9 fusion.111
  73.5 1.8 copy.124
  75.3 2.7 fusion.119
  78.0 2.6 fusion.118
  80.7 1.7 fusion.117
  82.4 1.7 fusion.116
  84.0 2.3 copy.94
  86.4 1.9 fusion.4
  90.4 1.0 convolution_bitcast_fusion.3
  91.5 1.0 convolution_bitcast_fusion.2
  92.5 1.0 convolution_bitcast_fusion.1
  93.6 2.3 copy.105
  96.0 2.7 fusion.23
  99.4 1.5 copy-done.3
  100.9 1.6 convolution_convert_fusion.block_ref
  102.5 15.7 %sum_over_tp.1 = f32[128,2048]{1,0:T(8,128)} custom-call(bf16[128,2048]{1,0:T(8,128)(2,1)} %convolution_convert_fusion.block_ref), custom_call_target="tpu_custom_call" | custom-call | tf_op jit(solution)/shard_map/sum_over_tp/pallas_call | solution.py:224
  118.2 1.5 fusion.25
  119.7 1.1 fusion.27
  120.8 1.3 fusion.121
  122.2 36.4 %all_gather.15 = f32[2048,16]{0,1:T(8,128)S(1)} all-gather(f32[128,16]{0,1:T(8,128)S(1)} %select_reduce_fusion), channel_id=1, replica_groups=mesh['seq'=16,'tp'=2] {'seq'}, dimensions={0}, use_global_device_ids=true | all-gather | bytes 139264 | tf_op jit(solution)/shard_map/all_gather | solution.py:330
  158.6 55.9 %all-gather.8.cloned.1.call-done = bf16[2048,2048]{1,0:T(8,128)(2,1)} async-done(((bf16[128,2048]{1,0:T(8,128)(2,1)}), bf16[2048,2048]{1,0:T(8,128)(2,1)}) %all-gather.8.cloned.1.call-update) | async-done | bytes 8388624 | tf_op jit(solution)/shard_map/all_gather | solution.py:332
  214.6 7.7 %fusion.2 = f32[2048,512]{1,0:T(8,128)S(1)} fusion(bf16[2048,2048]{1,0:T(8,128)(2,1)} %all-gather.8.cloned.1.call-done, bf16[1,2048,512]{2,1,0:T(8,128)(2,1)} %param.32), kind=kOutput, calls=%fused_computation.5 | convolution fusion | flops 4294967296 | bytes 14680064 | tf_op jit(solution)/shard_map/dot_general | solution.py:333
  222.3 5.2 %multiply_convert_fusion.1 = bf16[2048,512]{1,0:T(8,128)(2,1)S(1)} fusion(f32[2048,512]{1,0:T(8,128)S(1)} %fusion.2, bf16[2048,2048]{1,0:T(8,128)(2,1)S(1)} %copy-done.61, bf16[1,2048,512]{2,1,0:T(8,128)(2,1)S(1)} %copy-done.62), kind=kOutput, calls=%fused_computation.1 | convolution fusion | flops 4301258752 | bytes 16777216 | tf_op jit(solution)/shard_map/dot_general | solution.py:334
  227.4 6.8 %multiply_convert_fusion = bf16[2048,2048]{1,0:T(8,128)(2,1)} fusion(bf16[2048,512]{1,0:T(8,128)(2,1)S(1)} %multiply_convert_fusion.1, f32[2048]{0:T(1024)S(1)} %bitcast.219, bf16[1,512,2048]{2,1,0:T(8,128)(2,1)S(1)} %copy-done), kind=kOutput, calls=%fused_computation | convolution fusion | flops 4303355904 | bytes 12591104 | tf_op jit(solution)/shard_map/dot_general | solution.py:336
  234.3 103.1 %reduce-scatter.3.cloned.1.call-done = bf16[128,2048]{1,0:T(8,128)(2,1)} async-done(((bf16[2048,2048]{1,0:T(8,128)(2,1)}), bf16[128,2048]{1,0:T(8,128)(2,1)}) %reduce-scatter.3.cloned.1.call-update) | async-done | bytes 524304 | tf_op jit(solution)/shard_map/reduce_scatter | solution.py:337
  338.0 15.8 %reduce-scatter.5.cloned.1.call-done = bf16[128,1024]{1,0:T(8,128)(2,1)} async-done(((bf16[128,2048]{1,0:T(8,128)(2,1)}), bf16[128,1024]{1,0:T(8,128)(2,1)}) %reduce-scatter.5.cloned.1.call-update) | async-done | bytes 262160 | tf_op jit(solution)/shard_map/reduce_scatter | solution.py:338
  355.7 17.5 %last_rows.1 = bf16[8,1024]{1,0:T(8,128)(2,1)} custom-call(f32[8,1024]{1,0:T(8,128)} %fusion.87.chosen_ref, bf16[1,1024]{1,0:T(2,128)(2,1)} %reshape.611.gain_ref), custom_call_target="tpu_custom_call" | custom-call | tf_op jit(solution)/shard_map/last_rows/pallas_call | solution.py:116
  373.2 5.3 %fusion.122.logits_ref = f32[8,3144]{1,0:T(8,128)} fusion(bf16[8,1024]{1,0:T(8,128)(2,1)} %last_rows.1, bf16[1024,3144]{0,1:T(8,128)(2,1)} %param.37), kind=kOutput, calls=%fused_computation.208 | convolution fusion | flops 51511296 | bytes 6555904 | tf_op jit(solution)/shard_map/dot_general | solution.py:371
  378.4 15.6 %log_softmax.1 = f32[8,3144]{1,0:T(8,128)} custom-call(f32[8,3144]{1,0:T(8,128)} %fusion.122.logits_ref), custom_call_target="tpu_custom_call" | custom-call | tf_op jit(solution)/shard_map/log_softmax/pallas_call | solution.py:164
  394.0 1.5 copy.166
  (189 shorter events, 17.0 us)
Async XLA Ops:
  7.2 220.3 %copy-start = (bf16[1,512,2048]{2,1,0:T(8,128)(2,1)S(1)}, bf16[1,512,2048]{2,1,0:T(8,128)(2,1)}, u32[]{:S(2)}) copy-start(bf16[1,512,2048]{2,1,0:T(8,128)(2,1)} %param.34) | copy-start | bytes 6291460
  7.2 76.9 %all-gather.4.cloned.1.call-start = ((), (), s32[]{:S(2)}) async-start(), calls=%async_computation.2 | async-start | bytes 1114112 | tf_op jit(solution)/shard_map/all_gather | solution.py:296
  7.9 85.6 %all-gather.6.cloned.1.call-start = ((), (), s32[]{:S(2)}) async-start(), calls=%async_computation.3 | async-start | bytes 1114112 | tf_op jit(solution)/shard_map/all_gather | solution.py:297
  25.1 3.0 copy-start.60
  25.2 4.4 %copy-start.58 = (s32[8]{0:T(128)S(1)}, s32[8]{0:T(128)}, u32[]{:S(2)}) copy-start(s32[8]{0:T(128)} %param.28) | copy-start | bytes 100
  27.1 5.9 %copy-start.1 = (bf16[128,2048]{1,0:T(8,128)(2,1)S(1)}, bf16[128,2048]{1,0:T(8,128)(2,1)}, u32[]{:S(2)}) copy-start(bf16[128,2048]{1,0:T(8,128)(2,1)} %gather_columns.1) | copy-start | bytes 1572868
  28.3 3.8 copy-start.39
  29.0 3.1 copy-start.42
  31.9 4.1 %copy-start.4 = (bf16[128,8,128]{2,0,1:T(8,128)(2,1)}, bf16[128,8,128]{2,0,1:T(8,128)(2,1)S(1)}, u32[]{:S(2)}) copy-start(bf16[128,8,128]{2,0,1:T(8,128)(2,1)S(1)} %maximum_convert_fusion) | copy-start | bytes 786436
  32.9 3.0 copy-start.16
  36.8 34.9 %collective-permute-start = (bf16[128,2048]{1,0:T(8,128)(2,1)}, bf16[128,2048]{1,0:T(8,128)(2,1)}, u32[]{:S(2)}, u32[]{:S(2)}) collective-permute-start(bf16[128,2048]{1,0:T(8,128)(2,1)} %pad_maximum_fusion), channel_id=1, source_target_pairs={{0,2},{2,4},{4,6},{6,8},{8,10},{10,12},{12,14},{14,16},{16,18},{18... | collective-permute-start | bytes 1572872 | tf_op jit(solution)/shard_map/ppermute | solution.py:20
  38.9 19.7 %collective-permute-start.1 = (bf16[128,2048]{1,0:T(8,128)(2,1)}, bf16[128,2048]{1,0:T(8,128)(2,1)}, u32[]{:S(2)}, u32[]{:S(2)}) collective-permute-start(bf16[128,2048]{1,0:T(8,128)(2,1)} %pad_maximum_fusion), channel_id=1, source_target_pairs={{0,4},{2,6},{4,8},{6,10},{8,12},{10,14},{12,16},{14,18},{16,20},{1... | collective-permute-start | bytes 1572872 | tf_op jit(solution)/shard_map/ppermute | solution.py:20
  43.1 21.2 %collective-permute-start.2 = (bf16[128,2048]{1,0:T(8,128)(2,1)}, bf16[128,2048]{1,0:T(8,128)(2,1)}, u32[]{:S(2)}, u32[]{:S(2)}) collective-permute-start(bf16[128,2048]{1,0:T(8,128)(2,1)} %pad_maximum_fusion), channel_id=1, source_target_pairs={{0,6},{2,8},{4,10},{6,12},{8,14},{10,16},{12,18},{14,20},{16,22},{... | collective-permute-start | bytes 1572872 | tf_op jit(solution)/shard_map/ppermute | solution.py:20
  47.5 20.6 %collective-permute-start.3 = (bf16[128,2048]{1,0:T(8,128)(2,1)}, bf16[128,2048]{1,0:T(8,128)(2,1)}, u32[]{:S(2)}, u32[]{:S(2)}) collective-permute-start(bf16[128,2048]{1,0:T(8,128)(2,1)} %pad_maximum_fusion), channel_id=1, source_target_pairs={{0,8},{2,10},{4,12},{6,14},{8,16},{10,18},{12,20},{14,22},{16,24},... | collective-permute-start | bytes 1572872 | tf_op jit(solution)/shard_map/ppermute | solution.py:20
  51.0 163.5 %all-gather.8.cloned.1.call-start = ((), (), s32[]{:S(2)}) async-start(), calls=%async_computation.4 | async-start | bytes 8912896 | tf_op jit(solution)/shard_map/all_gather | solution.py:332
  66.2 9.1 %copy-start.7 = (bf16[128,8,128]{2,0,1:T(8,128)(2,1)S(1)}, bf16[128,8,128]{2,0,1:T(8,128)(2,1)}, u32[]{:S(2)}) copy-start(bf16[128,8,128]{2,0,1:T(8,128)(2,1)} %copy-done.6) | copy-start | bytes 786436
  75.3 5.3 %copy-start.23 = (bf16[16,8,8,128]{3,2,1,0:T(8,128)(2,1)S(1)}, bf16[16,8,8,128]{3,2,1,0:T(8,128)(2,1)}, u32[]{:S(2)}) copy-start(bf16[16,8,8,128]{3,2,1,0:T(8,128)(2,1)} %get-tuple-element.30) | copy-start | bytes 786436
  75.3 7.0 %copy-start.24 = (bf16[16,8,8,128]{3,2,1,0:T(8,128)(2,1)S(1)}, bf16[16,8,8,128]{3,2,1,0:T(8,128)(2,1)}, u32[]{:S(2)}) copy-start(bf16[16,8,8,128]{3,2,1,0:T(8,128)(2,1)} %get-tuple-element.31) | copy-start | bytes 786436
  86.4 2.6 copy-start.10
  88.9 2.6 copy-start.13
  89.1 3.5 copy-start.14
  91.5 4.3 %copy-start.33 = (f32[8,128]{1,0:T(8,128)S(1)}, f32[8,128]{1,0:T(8,128)}, u32[]{:S(2)}) copy-start(f32[8,128]{1,0:T(8,128)} %copy-done.32) | copy-start | bytes 12292
  92.5 3.3 copy-start.49
  92.5 3.3 copy-start.50
  95.8 2.9 copy-start.11
  95.8 2.9 copy-start.27
  95.9 2.9 copy-start.34
  95.9 3.1 copy-start.18
  95.9 3.1 copy-start.19
  95.9 3.1 copy-start.20
  95.9 3.1 copy-start.21
  95.9 3.1 copy-start.22
  95.9 3.1 copy-start.31
  95.9 3.1 copy-start.45
  95.9 3.1 copy-start.46
  95.9 3.1 copy-start.47
  96.0 3.1 copy-start.48
  102.5 17.2 %copy-start.29 = (f32[2048]{0:T(1024)S(1)}, f32[2048]{0:T(1024)}, u32[]{:S(2)}) copy-start(f32[2048]{0:T(1024)} %convert_element_type.128) | copy-start | bytes 24580
  118.1 2.7 copy-start.25
  118.2 4.0 copy-start.44
  120.8 216.6 %reduce-scatter.3.cloned.1.call-start = ((), (), s32[]{:S(2)}) async-start(), calls=%async_computation.5 | async-start | bytes 8912896 | tf_op jit(solution)/shard_map/reduce_scatter | solution.py:337
  214.5 7.7 %copy-start.61 = (bf16[2048,2048]{1,0:T(8,128)(2,1)S(1)}, bf16[2048,2048]{1,0:T(8,128)(2,1)}, u32[]{:S(2)}) copy-start(bf16[2048,2048]{1,0:T(8,128)(2,1)} %all-gather.8.cloned.1.call-done) | copy-start | bytes 25165828
  214.6 7.7 %copy-start.62 = (bf16[1,2048,512]{2,1,0:T(8,128)(2,1)S(1)}, bf16[1,2048,512]{2,1,0:T(8,128)(2,1)}, u32[]{:S(2)}) copy-start(bf16[1,2048,512]{2,1,0:T(8,128)(2,1)} %param.33) | copy-start | bytes 6291460
  234.3 103.2 %copy-start.57 = (bf16[1024]{0:T(1024)(128)(2,1)S(1)}, bf16[1024]{0:T(1024)(128)(2,1)}, u32[]{:S(2)}) copy-start(bf16[1024]{0:T(1024)(128)(2,1)} %param.36) | copy-start | bytes 6148
  234.3 120.6 %copy-start.41 = (s32[128]{0:T(128)S(1)}, s32[128]{0:T(128)}, u32[]{:S(2)}) copy-start(s32[128]{0:T(128)} %copy-done.39) | copy-start | bytes 1540
  234.3 120.6 %copy-start.52 = (s32[8]{0:T(128)S(1)}, s32[8]{0:T(128)}, u32[]{:S(2)}) copy-start(s32[8]{0:T(128)} %get-tuple-element.42) | copy-start | bytes 100
  234.3 119.5 %reduce-scatter.5.cloned.1.call-start = ((), (), s32[]{:S(2)}) async-start(), calls=%async_computation.6 | async-start | bytes 786432 | tf_op jit(solution)/shard_map/reduce_scatter | solution.py:338
  354.8 23.6 %copy-start.15 = (bf16[128,1024]{1,0:T(8,128)(2,1)}, bf16[128,1024]{1,0:T(8,128)(2,1)S(1)}, u32[]{:S(2)}) copy-start(bf16[128,1024]{1,0:T(8,128)(2,1)S(1)} %add_convert_fusion) | copy-start | bytes 786436
  (24 other events, 36.3 us)
Sparse Core Ops, SparseCore 0:
  10.2 40.5 all-gather.3
  53.0 37.9 all-gather.5
  120.9 93.6 all-gather.7
  234.4 102.9 reduce-scatter.2
  339.5 14.2 reduce-scatter.4

commit v3 on v2

--- a/solution.py
+++ b/solution.py
@@ -43,24 +43,6 @@
 def lookup(selector, table):
     hit = selector[:, None] == jnp.arange(table.shape[0])[None, :]
     return jnp.sum(jnp.where(hit, table[None, :], 0), 1)
-
-
-def attend(carry, query, keys, values, allowed):
-    best, total, accum = carry
-    heads = query.shape[1]
-    keys = keys.reshape(keys.shape[0], heads, -1)
-    values = values.reshape(values.shape[0], heads, -1)
-    scale = query.shape[-1] ** (-0.5)
-    scores = jnp.einsum("thd,khd->htk", query, keys, preferred_element_type=jnp.float32) * scale
-    scores = jnp.where(allowed[None], scores, NEGATIVE)
-    top = jnp.maximum(best, jnp.max(scores, -1))
-    factor = jnp.exp(best - top)
-    weights = jnp.where(allowed[None], jnp.exp(scores - top[..., None]), 0.0)
-    total = factor * total + jnp.sum(weights, -1)
-    accum = factor[..., None] * accum + jnp.einsum(
-        "htk,khd->htd", weights.astype(jnp.bfloat16), values, preferred_element_type=jnp.float32
-    )
-    return (top, total, accum)
 
 
 def partner(axis, bit):
@@ -235,6 +217,290 @@
         compiler_params=pltpu.CompilerParams(collective_id=4, has_side_effects=True),
         name="sum_over_tp",
     )(block)
+
+
+def bit(index, place):
+    return (index // (1 << place)) % 2
+
+
+def reversed_index(count):
+    me = lax.axis_index("seq")
+    return sum(bit(me, k) * (1 << (count - 1 - k)) for k in range(count))
+
+
+def advance(chains):
+    for turn in range(max(len(chain) for chain in chains)):
+        for chain in chains:
+            if turn < len(chain):
+                chain[turn]()
+
+
+def spread_rows(rows, share):
+    count = lax.axis_size("seq").bit_length() - 1
+    blocks = 1 << count
+    tall, wide = rows.shape
+    quarter = wide // 4
+    experts = share.shape[0]
+    stages = bits_of("seq") + bits_of("tp")
+    slots = 4 * count + 1
+
+    def kernel(rows_ref, share_ref, out_ref, share_out, send_sem, recv_sem):
+        place = reversed_index(count)
+        tp = lax.axis_index("tp")
+        out_ref[place] = rows_ref[...]
+        share_out[place] = share_ref[...]
+        greet(stages)
+        used = iter(range(slots))
+        flying = {}
+
+        def hop(name, stage, view):
+            def act():
+                if name in flying:
+                    flying[name].wait()
+                slot = next(used)
+                piece = view()
+                flying[name] = swap(piece, piece, send_sem.at[slot], recv_sem.at[slot], stage)
+
+            return act
+
+        def span_of(j):
+            return pl.ds((place // (1 << j)) * (1 << j), 1 << j)
+
+        def rows_view(j, start, size):
+            return lambda: out_ref.at[span_of(j), :, pl.ds(start, size)]
+
+        own = pl.multiple_of(tp * quarter, quarter)
+        crossing = [
+            hop("q", ("seq", count - 1 - j), rows_view(j, own, quarter)) for j in range(count - 1)
+        ]
+        crossing.append(hop("q", ("tp", 0), rows_view(count - 1, own, quarter)))
+        crossing.append(hop("q", ("seq", 0), rows_view(count - 1, 0, 2 * quarter)))
+        chains = [crossing]
+        for part in (2, 3):
+            chains.append([
+                hop(part, ("seq", count - 1 - j), rows_view(j, part * quarter, quarter))
+                for j in range(count)
+            ])
+        chains.append([
+            hop("s", ("seq", count - 1 - j), lambda j=j: share_out.at[span_of(j)])
+            for j in range(count)
+        ])
+        advance(chains)
+        for copy in flying.values():
+            copy.wait()
+
+    return pl.pallas_call(
+        kernel,
+        out_shape=(
+            jax.ShapeDtypeStruct((blocks, tall, wide), rows.dtype),
+            jax.ShapeDtypeStruct((blocks, experts, tall), share.dtype),
+        ),
+        in_specs=[pl.BlockSpec(memory_space=VMEM)] * 2,
+        out_specs=(pl.BlockSpec(memory_space=VMEM), pl.BlockSpec(memory_space=VMEM)),
+        scratch_shapes=[pltpu.SemaphoreType.DMA((slots,)), pltpu.SemaphoreType.DMA((slots,))],
+        compiler_params=pltpu.CompilerParams(
+            collective_id=5, has_side_effects=True, vmem_limit_bytes=40 << 20
+        ),
+        name="spread_rows",
+    )(rows, share)
+
+
+def collect_rows(partial):
+    blocks, tall, wide = partial.shape
+    count = blocks.bit_length() - 1
+    half = wide // 2
+    groups = 4
+    w = half // groups
+    stages = bits_of("seq") + bits_of("tp")
+    slots = groups * (2 * count + 1)
+
+    def kernel(part_ref, out_ref, *rest):
+        buffers, (send_sem, recv_sem) = iter(rest[:-2]), rest[-2:]
+        greet(stages)
+        me, tp = lax.axis_index("seq"), lax.axis_index("tp")
+        used = iter(range(slots))
+
+        def send(source, target, stage):
+            slot = next(used)
+            return swap(source, target, send_sem.at[slot], recv_sem.at[slot], stage)
+
+        def add(size, mine, base, got, out):
+            def body(i, _):
+                total = mine[base + i].astype(jnp.float32) + got[i].astype(jnp.float32)
+                out[i] = total.astype(jnp.bfloat16)
+                return 0
+
+            lax.fori_loop(0, size, body, 0)
+
+        def scatter(state, j):
+            size = 1 << (count - 1 - j)
+            got, out = next(buffers), next(buffers)
+            mine = bit(me, j)
+            source = state
+            copy = send(source.at[pl.ds((1 - mine) * size, size)], got, ("seq", j))
+
+            def end():
+                copy.wait()
+                add(size, source, mine * size, got, out)
+                return out
+
+            return end
+
+        def straight(group):
+            ends, states = {}, {}
+            views = [part_ref.at[:, :, pl.ds(h * half + group * w, w)] for h in range(2)]
+
+            def step(j):
+                def act():
+                    for h in range(2):
+                        state = views[h] if j == 0 else ends[h]()
+                        ends[h] = scatter(state, j)
+
+                return act
+
+            def cross():
+                both, got = next(buffers), next(buffers)
+                for h in range(2):
+                    both[h] = ends[h]()[0]
+                states["both"], states["got"] = both, got
+                states["copy"] = send(both.at[1 - tp], got, ("tp", 0))
+
+            def finish():
+                states["copy"].wait()
+                out_ref[:, group * w : (group + 1) * w] = states["both"][tp].astype(
+                    jnp.float32
+                ) + states["got"][...].astype(jnp.float32)
+
+            return [step(j) for j in range(count)] + [cross, finish]
+
+        def crossing(group):
+            ends, states = {}, {}
+            size = blocks // 2
+
+            def first():
+                for h in range(2):
+                    got = next(buffers)
+                    mine = bit(me, 0)
+                    view = part_ref.at[:, :, pl.ds(h * half + group * w, w)]
+                    copy = send(view.at[pl.ds((1 - mine) * size, size)], got, ("seq", 0))
+                    states[h] = (view, mine, got, copy)
+                states["both"] = next(buffers)
+
+            def cross():
+                both, got = states["both"], next(buffers)
+                for h in range(2):
+                    view, mine, landed, copy = states[h]
+                    copy.wait()
+                    add(size, view, mine * size, landed, both.at[h])
+                states["got"] = got
+                states["copy"] = send(both.at[1 - tp], got, ("tp", 0))
+
+            def second():
+                states["copy"].wait()
+                out = next(buffers)
+                add(size, states["both"].at[tp], 0, states["got"], out)
+                ends[0] = scatter(out, 1)
+
+            def step(j):
+                def act():
+                    ends[0] = scatter(ends[0](), j)
+
+                return act
+
+            def finish():
+                out_ref[:, group * w : (group + 1) * w] = ends[0]()[0].astype(jnp.float32)
+
+            return [first, cross, second] + [step(j) for j in range(2, count)] + [finish]
+
+        advance([crossing(g) if g < groups // 2 else straight(g) for g in range(groups)])
+
+    def shapes():
+        bf16 = jnp.bfloat16
+        listing = []
+
+        def scatter(j):
+            size = 1 << (count - 1 - j)
+            listing.extend([VMEM((size, tall, w), bf16)] * 2)
+
+        def straight():
+            cross = [VMEM((2, tall, w), bf16), VMEM((tall, w), bf16)]
+            return [lambda j=j: (scatter(j), scatter(j)) for j in range(count)] + [
+                lambda: listing.extend(cross), lambda: None
+            ]
+
+        def crossing():
+            size = blocks // 2
+            block = VMEM((size, tall, w), bf16)
+            pair = VMEM((2, size, tall, w), bf16)
+            return [
+                lambda: listing.extend([block, block, pair]),
+                lambda: listing.extend([block]),
+                lambda: (listing.extend([block]), scatter(1)),
+            ] + [lambda j=j: scatter(j) for j in range(2, count)] + [lambda: None]
+
+        advance([crossing() if g < groups // 2 else straight() for g in range(groups)])
+        return listing
+
+    return pl.pallas_call(
+        kernel,
+        out_shape=jax.ShapeDtypeStruct((tall, half), jnp.float32),
+        in_specs=[pl.BlockSpec(memory_space=VMEM)],
+        out_specs=pl.BlockSpec(memory_space=VMEM),
+        scratch_shapes=shapes()
+        + [pltpu.SemaphoreType.DMA((slots,)), pltpu.SemaphoreType.DMA((slots,))],
+        compiler_params=pltpu.CompilerParams(
+            collective_id=6, has_side_effects=True, vmem_limit_bytes=56 << 20
+        ),
+        name="collect_rows",
+    )(partial)
+
+
+def attention(query, prefix_keys, prefix_values, suffix, bias):
+    tall, wide = query.shape
+    heads = wide // HD
+    cached = prefix_keys.shape[0]
+    keys = bias.shape[1]
+    many = len(suffix)
+    scale = HD ** (-0.5)
+
+    def kernel(query_ref, cached_k, cached_v, bias_ref, *rest):
+        suffix_k, suffix_v, out_ref = rest[:many], rest[many : 2 * many], rest[2 * many]
+        head = query_ref[...]
+        scores = [
+            lax.dot_general(
+                head, block[...], (((1,), (1,)), ((), ())), preferred_element_type=jnp.float32
+            )
+            for block in (cached_k, *suffix_k)
+        ]
+        scores = jnp.concatenate(scores, 1) * scale + bias_ref[...]
+        weights = jnp.exp(scores - jnp.max(scores, -1, keepdims=True))
+        total = jnp.sum(weights, -1, keepdims=True)
+        weights = weights.astype(jnp.bfloat16)
+        summed = jnp.dot(weights[:, :cached], cached_v[...], preferred_element_type=jnp.float32)
+        for n, block in enumerate(suffix_v):
+            start = cached + n * tall
+            summed += jnp.dot(
+                weights[:, start : start + tall], block[...], preferred_element_type=jnp.float32
+            )
+        out_ref[...] = (summed / total).astype(jnp.bfloat16)
+
+    def column(rows, offset):
+        return pl.BlockSpec((rows, HD), lambda h: (0, h + offset))
+
+    return pl.pallas_call(
+        kernel,
+        out_shape=jax.ShapeDtypeStruct((tall, wide), jnp.bfloat16),
+        grid=(heads,),
+        in_specs=[column(tall, 0), column(cached, 0), column(cached, 0)]
+        + [pl.BlockSpec((tall, keys), lambda h: (0, 0))]
+        + [column(tall, 0)] * many
+        + [column(tall, heads)] * many,
+        out_specs=column(tall, 0),
+        cost_estimate=pl.CostEstimate(
+            flops=4 * tall * keys * wide, bytes_accessed=4 * keys * wide, transcendentals=0
+        ),
+        name="attention",
+    )(query, prefix_keys, prefix_values, bias, *suffix, *suffix)
 
 
 def on_device(
@@ -287,11 +553,6 @@
     ).astype(bf16)
     key_rows = key_rows.reshape(tok_dev, heads * HD)
     value_rows = jnp.dot(normed, w_value, preferred_element_type=f32).astype(bf16)
-    start_state = (
-        jnp.full((heads, tok_dev), NEGATIVE, f32),
-        jnp.zeros((heads, tok_dev), f32),
-        jnp.zeros((heads, tok_dev, HD), f32),
-    )
     pieces = (
         lax.all_gather(prefix_keys, "seq", axis=0, tiled=True),
         lax.all_gather(prefix_values, "seq", axis=0, tiled=True),
@@ -300,23 +561,20 @@
     shard_ids = jnp.arange(count) // shard_rows
     key_group = lookup(shard_ids, shard_group)
     fold_allowed = own_group[:, None] == key_group[None, :]
-    state = attend(start_state, query, pieces[0], pieces[1], fold_allowed)
     own_allowed = (own_request[:, None] == own_request[None, :]) & (
         local_index[None, :] <= local_index[:, None]
     )
-    state = attend(state, query, key_rows, value_rows, own_allowed)
     both_rows = jnp.concatenate([key_rows, value_rows], 1)
-    behind = [from_behind(both_rows, "seq", step) for step in range(1, SPAN + 1)]
-    half = heads * HD
+    suffix = [both_rows] + [from_behind(both_rows, "seq", step) for step in range(1, SPAN + 1)]
+    permitted = [fold_allowed, own_allowed]
     for step in range(1, SPAN + 1):
-        moving = behind[step - 1]
         key_index = (seq_index - step) * tok_dev + jnp.arange(tok_dev)
         key_request = request_of(key_index, ends)
-        allowed = (key_index >= 0)[None, :] & (own_request[:, None] == key_request[None, :])
-        state = attend(state, query, moving[:, :half], moving[:, half:], allowed)
-    best, total, accum = state
-    attended = (accum / total[..., None]).astype(bf16)
-    attended = jnp.transpose(attended, (1, 0, 2)).reshape(tok_dev, heads * HD)
+        permitted.append(
+            (key_index >= 0)[None, :] & (own_request[:, None] == key_request[None, :])
+        )
+    bias = jnp.where(jnp.concatenate(permitted, 1), 0.0, NEGATIVE)
+    attended = attention(query.reshape(tok_dev, heads * HD), *pieces, suffix, bias)
     mixed = jnp.dot(attended, w_out, preferred_element_type=f32).astype(bf16)
     resid_full = (full_x.astype(f32) + sum_over_tp(mixed)).astype(bf16)
     moe_in = normalize(resid_full.astype(f32), moe_gain).astype(bf16)
@@ -324,18 +582,17 @@
     experts = w_router.shape[1]
     topk = routes.shape[1]
     probs = jax.nn.softmax(jnp.dot(moe_in, w_router, preferred_element_type=f32), -1)
-    if 2 * topk >= experts:
+    if 2 * topk >= experts and tp_count == 2:
         named = routes[:, :, None] == jnp.arange(experts)[None, None, :]
         share = jnp.sum(jnp.where(named, probs[:, None, :], 0.0), 1)
-        shares = lax.all_gather(share, "seq", axis=0, tiled=True)
-        own_share = lax.dynamic_slice_in_dim(shares, seq_index, 1, 1)
-        rows = lax.all_gather(moe_in, "seq", axis=0, tiled=True)
+        blocks, shares = spread_rows(moe_in, share.T)
+        own_share = lax.dynamic_slice_in_dim(shares, seq_index, 1, 1).reshape(-1, 1)
+        rows = blocks.reshape(-1, width)
         gate = jnp.dot(rows, w_gate[0], preferred_element_type=f32)
         up = jnp.dot(rows, w_up[0], preferred_element_type=f32)
         act = (jax.nn.silu(gate) * up).astype(bf16)
         partial_out = (jnp.dot(act, w_down[0], preferred_element_type=f32) * own_share).astype(bf16)
-        summed = lax.psum_scatter(partial_out, "seq", scatter_dimension=0, tiled=True)
-        moe_part = lax.psum_scatter(summed, "tp", scatter_dimension=1, tiled=True).astype(f32)
+        moe_part = collect_rows(partial_out.reshape(seq_count, tok_dev, width))
     else:
         flat = routes.reshape(-1)
         hits = (flat[:, None] == jnp.arange(experts)[None, :]).astype(jnp.int32)

time: 403 us -> 326 us (0.81)
  Pallas kernels: 59.8 us -> 204 us
  waiting for transfers between devices: 179 us -> 38.1 us
  blocking collectives: 36.4 us -> 0 us
  matrix products: 56.6 us -> 31.5 us
  local copies, waits for them, and re-layouts: 27.1 us -> 5.69 us
    pallas_call x0 -> x3, Pallas kernels: none -> 144 us  [the longest x1 69 us: collect_rows(): pl.pallas_call(kernel, out_shape=jax.ShapeDtypeStruct((tall, half), jnp.f...]
    reduce_scatter x2 -> x0, waiting for transfers between devices: 119 us -> none  [the longest x1 103 us: on_device(): lax.psum_scatter(partial_out, 'seq', scatter_dimension=0, tiled=True)]
    all_gather x1 -> x0, waiting for transfers between devices: 55.9 us -> none  [on_device(): rows = lax.all_gather(moe_in, 'seq', axis=0, tiled=True)]
    all_gather x1 -> x0, blocking collectives: 36.4 us -> none  [on_device(): shares = lax.all_gather(share, 'seq', axis=0, tiled=True)]
    all_gather x1, waiting for transfers between devices: 0.01 us -> 35.9 us  [on_device(): lax.all_gather(prefix_values, 'seq', axis=0, tiled=True)]
    dot_general x12 -> x0, matrix products: 17.9 us -> none  [the longest x6 11.5 us: attend(): jnp.einsum('thd,khd->htk', query, keys, preferred_element_type=jnp.float32)]
    reshape x5 -> x0, local copies, waits for them, and re-layouts: 7.11 us -> none  [attend(): values = values.reshape(values.shape[0], heads, -1)]
    slice x5 -> x0, local copies, waits for them, and re-layouts: 6.41 us -> none  [the longest x3 5.46 us: on_device(): state = attend(state, query, moving[:, :half], moving[:, half:], allowed)]
  transfers between devices with their start and end apart: 9 -> 6, of which waited for: 4 -> 2; matrix products, arithmetic and copies ran while one was open for 14% -> 7% of each run, Pallas kernels for 3% -> 3%
where the time goes in v3:
time: 326 us; the launch traced here: 325 us
  Pallas kernels  204 us (63%)
  waiting for transfers between devices  38.1 us (12%)
  matrix products  31.5 us (10%)
  other arithmetic  17.9 us (5%)
  between operations  14.5 us (4%)
  starting transfers between devices  14 us (4%)
  local copies, waits for them, and re-layouts  5.69 us (2%)
    pallas_call x1, Pallas kernels, collect_rows(): pl.pallas_call(kernel, out_shape=jax.ShapeDtypeStruct((tall, half), jnp.f...  69 us
    pallas_call x1, Pallas kernels, spread_rows(): pl.pallas_call(kernel, out_shape=(jax.ShapeDtypeStruct((blocks, tall, wid...  66.5 us
    all_gather x1, waiting for transfers between devices, on_device(): lax.all_gather(prefix_values, 'seq', axis=0, tiled=True)  35.9 us
    pallas_call x1, Pallas kernels, log_softmax(): pl.pallas_call(kernel, out_shape=jax.ShapeDtypeStruct((rows, part), jnp.f...  16.7 us
    pallas_call x1, Pallas kernels, sum_over_tp(): pl.pallas_call(kernel, out_shape=jax.ShapeDtypeStruct((rows, part), jnp.f...  16.2 us
    pallas_call x1, Pallas kernels, last_rows(): pl.pallas_call(kernel, out_shape=jax.ShapeDtypeStruct((rows, part), jnp.b...  15.2 us
    ppermute x4, starting transfers between devices, from_behind(): lax.ppermute(value, axis, [(source, source + steps) for source in range(l...  13.9 us
    pallas_call x1, Pallas kernels, gather_columns(): pl.pallas_call(kernel, out_shape=jax.ShapeDtypeStruct((rows, part * count...  11.1 us
  transfers between devices with their start and end apart: 6, of which 2 were waited for; matrix products, arithmetic and copies ran while one was open for 7% of the time, Pallas kernels for 3%

profile of v3, /device:TPU:0, one launch (start us, length us, event | category | flops | bytes accessed | tf_op | source)
XLA Modules:
  0.0 325.4 jit_solution(16132035361028936726)
XLA Ops:
  7.2 0.7 all-gather.3.cloned.1.call-update
  8.0 0.7 convert_element_type.82
  8.7 11.1 %gather_columns.1 = bf16[128,2048]{1,0:T(8,128)(2,1)} custom-call(bf16[128,1024]{1,0:T(8,128)(2,1)} %block_ref.1), custom_call_target="tpu_custom_call" | custom-call | tf_op jit(solution)/shard_map/gather_columns/pallas_call | solution.py:179
  19.8 1.4 fusion.7
  21.2 3.3 %convolution_bitcast_fusion = f32[16,8,8,128]{3,1,2,0:T(8,128)S(1)} fusion(bf16[2048,1024]{1,0:T(8,128)(2,1)} %param.22, bf16[128,2048]{1,0:T(8,128)(2,1)} %gather_columns.1, f32[2048]{0:T(1024)S(1)} %convert_element_type.82, f32[128]{0:T(128)S(1)} %add_rsqrt_fusion.1), kind=kOutput, calls=%fused_computation.12 | convolution fusion | flops 537919488 | bytes 5251584 | tf_op jit(solution)/shard_map/dot_general | solution.py:552
  24.6 0.8 convolution_bitcast_fusion.1
  25.4 0.9 copy.23
  26.4 0.2 reduce-window.7
  26.6 0.6 convert_reduce_fusion
  27.2 0.5 broadcast_add_fusion
  27.7 0.6 select_reduce_fusion.2
  28.4 0.3 multiply_cosine_fusion
  28.7 2.4 subtract_convert_fusion
  31.3 0.8 convolution_convert_fusion.1
  32.2 4.5 %collective-permute-start.3 = (bf16[128,2048]{1,0:T(8,128)(2,1)S(1)}, bf16[128,2048]{1,0:T(8,128)(2,1)}, u32[]{:S(2)}, u32[]{:S(2)}) collective-permute-start(bf16[128,2048]{1,0:T(8,128)(2,1)S(1)} %pad_maximum_fusion.rest_0_.rest_5_), channel_id=1, source_target_pairs={{0,8},{2,10},{4,12},{6,14},{8,16},{10,18},{12,20},{14,22},{16,24},... | collective-permute-start | bytes 1572872 | tf_op jit(solution)/shard_map/ppermute | solution.py:20
  36.7 2.5 collective-permute-start.2
  39.2 3.8 %collective-permute-start.1 = (bf16[128,2048]{1,0:T(8,128)(2,1)S(1)}, bf16[128,2048]{1,0:T(8,128)(2,1)}, u32[]{:S(2)}, u32[]{:S(2)}) collective-permute-start(bf16[128,2048]{1,0:T(8,128)(2,1)S(1)} %pad_maximum_fusion.rest_0_.rest_5_), channel_id=1, source_target_pairs={{0,4},{2,6},{4,8},{6,10},{8,12},{10,14},{12,16},{14,18},{16,20},{1... | collective-permute-start | bytes 1572872 | tf_op jit(solution)/shard_map/ppermute | solution.py:20
  43.0 3.1 collective-permute-start
  46.2 0.8 compare_dynamic-update-slice_fusion
  47.0 0.8 and_dynamic-update-slice_fusion.4
  47.8 0.7 and_dynamic-update-slice_fusion.3
  48.6 0.7 and_dynamic-update-slice_fusion.2
  49.3 0.7 and_dynamic-update-slice_fusion.1
  50.0 0.8 and_dynamic-update-slice_fusion
  50.8 1.8 pad_maximum_fusion.1
  52.6 1.3 reshape.205.gain_ref
  53.9 0.7 convert_element_type.98
  54.5 1.7 copy.30
  56.3 0.9 broadcast_select_fusion.bias_ref
  57.1 1.5 collective-permute-done.1.rest_2_.rest_7_
  58.6 35.9 %all-gather.5.cloned.1.call-done.cached_v = bf16[512,1024]{1,0:T(8,128)(2,1)} async-done(((bf16[32,1024]{1,0:T(8,128)(2,1)}), bf16[512,1024]{1,0:T(8,128)(2,1)}) %all-gather.5.cloned.1.call-update) | async-done | bytes 1048592 | tf_op jit(solution)/shard_map/all_gather | solution.py:558
  94.5 9.0 %attention.1 = bf16[128,1024]{1,0:T(8,128)(2,1)} custom-call(bf16[128,1024]{1,0:T(8,128)(2,1)} %bitcast.50, bf16[512,1024]{1,0:T(8,128)(2,1)} %all-gather.3.cloned.1.call-done.cached_k, bf16[512,1024]{1,0:T(8,128)(2,1)} %all-gather.5.cloned.1.call-done.cached_v, f32[128,1152]{1,0:T(8,128)} %broadcast_select_fusion.bias_ref, bf16[128,2048]{1,0:T(8,128)(2,1)} %copy-done.2, ...), custom_call_target="tpu_custom_call" | custom-call | flops 603979776 | bytes 4718592 | tf_op jit(solution)/shard_map/attention/pallas_call | solution.py:490
  103.5 3.8 %convolution_convert_fusion.block_ref = bf16[128,2048]{1,0:T(8,128)(2,1)} fusion(bf16[128,1024]{1,0:T(8,128)(2,1)} %attention.1, bf16[1024,2048]{1,0:T(8,128)(2,1)} %param.24), kind=kOutput, calls=%fused_computation.2 | convolution fusion | flops 537133056 | bytes 4980736 | tf_op jit(solution)/shard_map/dot_general | solution.py:578
  107.4 16.2 %sum_over_tp.1 = f32[128,2048]{1,0:T(8,128)} custom-call(bf16[128,2048]{1,0:T(8,128)(2,1)} %convolution_convert_fusion.block_ref), custom_call_target="tpu_custom_call" | custom-call | tf_op jit(solution)/shard_map/sum_over_tp/pallas_call | solution.py:206
  123.6 1.6 fusion.4
  125.3 0.2 fusion.6.rows_ref
  125.5 0.3 fusion.24
  125.8 66.5 %spread_rows.1 = (bf16[16,128,2048]{2,1,0:T(8,128)(2,1)S(1)}, f32[16,16,128]{2,1,0:T(8,128)S(1)}) custom-call(bf16[128,2048]{1,0:T(8,128)(2,1)S(1)} %fusion.6.rows_ref, f32[16,128]{1,0:T(8,128)S(1)} %bitcast.44), custom_call_target="tpu_custom_call" | custom-call | tf_op jit(solution)/shard_map/spread_rows/pallas_call | solution.py:292
  192.3 4.5 %fusion.2 = f32[2048,512]{1,0:T(8,128)S(1)} fusion(bf16[2048,2048]{1,0:T(8,128)(2,1)S(1)} %bitcast.45, bf16[1,2048,512]{2,1,0:T(8,128)(2,1)S(1)} %copy-done.15), kind=kOutput, calls=%fused_computation.5 | convolution fusion | flops 4294967296 | bytes 14680064 | tf_op jit(solution)/shard_map/dot_general | solution.py:591
  196.9 5.1 %multiply_convert_fusion.1 = bf16[2048,512]{1,0:T(8,128)(2,1)S(1)} fusion(f32[2048,512]{1,0:T(8,128)S(1)} %fusion.2, bf16[2048,2048]{1,0:T(8,128)(2,1)S(1)} %bitcast.46, bf16[1,2048,512]{2,1,0:T(8,128)(2,1)S(1)} %copy-done.16), kind=kOutput, calls=%fused_computation.1 | convolution fusion | flops 4301258752 | bytes 16777216 | tf_op jit(solution)/shard_map/dot_general | solution.py:592
  202.0 6.8 %multiply_convert_fusion = bf16[2048,2048]{1,0:T(8,128)(2,1)} fusion(bf16[2048,512]{1,0:T(8,128)(2,1)S(1)} %multiply_convert_fusion.1, f32[2048]{0:T(1024)S(1)} %bitcast.54, bf16[1,512,2048]{2,1,0:T(8,128)(2,1)S(1)} %copy-done), kind=kOutput, calls=%fused_computation | convolution fusion | flops 4303355904 | bytes 12591104 | tf_op jit(solution)/shard_map/dot_general | solution.py:594
  208.8 69.0 %collect_rows.1 = f32[128,1024]{1,0:T(8,128)} custom-call(bf16[16,128,2048]{2,1,0:T(8,128)(2,1)} %bitcast.47), custom_call_target="tpu_custom_call" | custom-call | tf_op jit(solution)/shard_map/collect_rows/pallas_call | solution.py:444
  277.8 1.1 add_convert_fusion
  279.0 0.8 fusion.13.chosen_ref
  279.8 15.2 %last_rows.1 = bf16[8,1024]{1,0:T(8,128)(2,1)} custom-call(f32[8,1024]{1,0:T(8,128)} %fusion.13.chosen_ref, bf16[1,1024]{1,0:T(2,128)(2,1)} %reshape.205.gain_ref), custom_call_target="tpu_custom_call" | custom-call | tf_op jit(solution)/shard_map/last_rows/pallas_call | solution.py:98
  295.0 5.3 %fusion.25.logits_ref = f32[8,3144]{1,0:T(8,128)} fusion(bf16[8,1024]{1,0:T(8,128)(2,1)} %last_rows.1, bf16[1024,3144]{0,1:T(8,128)(2,1)} %param.37), kind=kOutput, calls=%fused_computation.84 | convolution fusion | flops 51511296 | bytes 6555904 | tf_op jit(solution)/shard_map/dot_general | solution.py:628
  300.3 16.7 %log_softmax.1 = f32[8,3144]{1,0:T(8,128)} custom-call(f32[8,3144]{1,0:T(8,128)} %fusion.25.logits_ref), custom_call_target="tpu_custom_call" | custom-call | tf_op jit(solution)/shard_map/log_softmax/pallas_call | solution.py:146
  317.0 1.5 copy.37
  (60 shorter events, 0.7 us)
Async XLA Ops:
  7.2 194.8 %copy-start = (bf16[1,512,2048]{2,1,0:T(8,128)(2,1)S(1)}, bf16[1,512,2048]{2,1,0:T(8,128)(2,1)}, u32[]{:S(2)}) copy-start(bf16[1,512,2048]{2,1,0:T(8,128)(2,1)} %param.34) | copy-start | bytes 6291460
  7.2 51.5 %all-gather.3.cloned.1.call-start = ((), (), s32[]{:S(2)}) async-start(), calls=%async_computation | async-start | bytes 1114112 | tf_op jit(solution)/shard_map/all_gather | solution.py:557
  7.9 86.6 %all-gather.5.cloned.1.call-start = ((), (), s32[]{:S(2)}) async-start(), calls=%async_computation.1 | async-start | bytes 1114112 | tf_op jit(solution)/shard_map/all_gather | solution.py:558
  19.8 4.9 %copy-start.1 = (bf16[128,2048]{1,0:T(8,128)(2,1)S(1)}, bf16[128,2048]{1,0:T(8,128)(2,1)}, u32[]{:S(2)}) copy-start(bf16[128,2048]{1,0:T(8,128)(2,1)} %gather_columns.1) | copy-start | bytes 1572868
  19.8 4.9 %copy-start.4 = (bf16[2048,1024]{1,0:T(8,128)(2,1)S(1)}, bf16[2048,1024]{1,0:T(8,128)(2,1)}, u32[]{:S(2)}) copy-start(bf16[2048,1024]{1,0:T(8,128)(2,1)} %param.21) | copy-start | bytes 12582916
  24.5 1.9 copy-start.14
  24.5 3.2 copy-start.12
  26.5 4.8 %copy-start.3 = (bf16[2048,1024]{1,0:T(8,128)(2,1)S(1)}, bf16[2048,1024]{1,0:T(8,128)(2,1)}, u32[]{:S(2)}) copy-start(bf16[2048,1024]{1,0:T(8,128)(2,1)} %param.23) | copy-start | bytes 12582916
  26.6 2.1 copy-start.8
  27.2 1.5 copy-start.7
  31.1 15.0 %copy-start.13 = (s32[16]{0:T(128)S(1)}, s32[16]{0:T(128)}, u32[]{:S(2)}) copy-start(s32[16]{0:T(128)} %param.27) | copy-start | bytes 196
  32.1 62.4 %copy-start.2 = (bf16[128,2048]{1,0:T(8,128)(2,1)}, bf16[128,2048]{1,0:T(8,128)(2,1)S(1)}, u32[]{:S(2)}) copy-start(bf16[128,2048]{1,0:T(8,128)(2,1)S(1)} %pad_maximum_fusion.rest_0_.rest_5_) | copy-start | bytes 1572868
  32.2 25.0 %collective-permute-start.3 = (bf16[128,2048]{1,0:T(8,128)(2,1)S(1)}, bf16[128,2048]{1,0:T(8,128)(2,1)}, u32[]{:S(2)}, u32[]{:S(2)}) collective-permute-start(bf16[128,2048]{1,0:T(8,128)(2,1)S(1)} %pad_maximum_fusion.rest_0_.rest_5_), channel_id=1, source_target_pairs={{0,8},{2,10},{4,12},{6,14},{8,16},{10,18},{12,20},{14,22},{16,24},... | collective-permute-start | bytes 1572872 | tf_op jit(solution)/shard_map/ppermute | solution.py:20
  36.7 20.5 %collective-permute-start.2 = (bf16[128,2048]{1,0:T(8,128)(2,1)S(1)}, bf16[128,2048]{1,0:T(8,128)(2,1)}, u32[]{:S(2)}, u32[]{:S(2)}) collective-permute-start(bf16[128,2048]{1,0:T(8,128)(2,1)S(1)} %pad_maximum_fusion.rest_0_.rest_5_), channel_id=1, source_target_pairs={{0,6},{2,8},{4,10},{6,12},{8,14},{10,16},{12,18},{14,20},{16,22},{... | collective-permute-start | bytes 1572872 | tf_op jit(solution)/shard_map/ppermute | solution.py:20
  39.2 19.4 %collective-permute-start.1 = (bf16[128,2048]{1,0:T(8,128)(2,1)S(1)}, bf16[128,2048]{1,0:T(8,128)(2,1)}, u32[]{:S(2)}, u32[]{:S(2)}) collective-permute-start(bf16[128,2048]{1,0:T(8,128)(2,1)S(1)} %pad_maximum_fusion.rest_0_.rest_5_), channel_id=1, source_target_pairs={{0,4},{2,6},{4,8},{6,10},{8,12},{10,14},{12,16},{14,18},{16,20},{1... | collective-permute-start | bytes 1572872 | tf_op jit(solution)/shard_map/ppermute | solution.py:20
  43.0 15.7 %collective-permute-start = (bf16[128,2048]{1,0:T(8,128)(2,1)S(1)}, bf16[128,2048]{1,0:T(8,128)(2,1)}, u32[]{:S(2)}, u32[]{:S(2)}) collective-permute-start(bf16[128,2048]{1,0:T(8,128)(2,1)S(1)} %pad_maximum_fusion.rest_0_.rest_5_), channel_id=1, source_target_pairs={{0,2},{2,4},{4,6},{6,8},{8,10},{10,12},{12,14},{14,16},{16,18},{18... | collective-permute-start | bytes 1572872 | tf_op jit(solution)/shard_map/ppermute | solution.py:20
  103.5 22.0 %copy-start.6 = (bf16[2048,16]{0,1:T(8,128)(2,1)S(1)}, bf16[2048,16]{0,1:T(8,128)(2,1)}, u32[]{:S(2)}) copy-start(bf16[2048,16]{0,1:T(8,128)(2,1)} %param.31) | copy-start | bytes 196612
  103.5 22.3 %copy-start.10 = (s32[128,8]{0,1:T(8,128)S(1)}, s32[128,8]{0,1:T(8,128)}, u32[]{:S(2)}) copy-start(s32[128,8]{0,1:T(8,128)} %param.35) | copy-start | bytes 12292
  123.6 68.7 %copy-start.15 = (bf16[1,2048,512]{2,1,0:T(8,128)(2,1)S(1)}, bf16[1,2048,512]{2,1,0:T(8,128)(2,1)}, u32[]{:S(2)}) copy-start(bf16[1,2048,512]{2,1,0:T(8,128)(2,1)} %param.32) | copy-start | bytes 6291460
  192.3 4.5 %copy-start.16 = (bf16[1,2048,512]{2,1,0:T(8,128)(2,1)S(1)}, bf16[1,2048,512]{2,1,0:T(8,128)(2,1)}, u32[]{:S(2)}) copy-start(bf16[1,2048,512]{2,1,0:T(8,128)(2,1)} %param.33) | copy-start | bytes 6291460
  208.8 70.2 %copy-start.9 = (s32[128]{0:T(128)S(1)}, s32[128]{0:T(128)}, u32[]{:S(2)}) copy-start(s32[128]{0:T(128)} %copy-done.8) | copy-start | bytes 1540
  208.8 70.2 %copy-start.11 = (s32[8]{0:T(128)S(1)}, s32[8]{0:T(128)}, u32[]{:S(2)}) copy-start(s32[8]{0:T(128)} %get-tuple-element.23) | copy-start | bytes 100
  278.9 39.6 %copy-start.5 = (bf16[128,1024]{1,0:T(8,128)(2,1)}, bf16[128,1024]{1,0:T(8,128)(2,1)S(1)}, u32[]{:S(2)}) copy-start(bf16[128,1024]{1,0:T(8,128)(2,1)S(1)} %add_convert_fusion) | copy-start | bytes 786436
Sparse Core Ops, SparseCore 0:
  10.2 40.6 all-gather.2
  53.0 41.4 all-gather.4

commit v4 on v3

--- a/solution.py
+++ b/solution.py
@@ -1,3 +1,4 @@
+import heapq
 import jax
 import jax.numpy as jnp
 from jax import lax
@@ -161,30 +162,60 @@
     )(logits)
 
 
-def gather_columns(block):
+def gather_front(block, *cached):
     stages = bits_of("tp")
     rows, part = block.shape
-    count = lax.axis_size("tp")
-
-    def kernel(block_ref, out_ref, send_sem, recv_sem):
-        greet(stages)
+    tp_count = lax.axis_size("tp")
+    count = lax.axis_size("seq").bit_length() - 1
+    many = len(cached)
+    slots = many * count + len(stages)
+
+    def kernel(block_ref, *rest):
+        cached_refs, out_ref, outs = rest[:many], rest[many], rest[many + 1 : 2 * many + 1]
+        send_sem, recv_sem = rest[-2:]
         me = lax.axis_index("tp")
+        place = reversed_index(count)
         out_ref[:, pl.ds(pl.multiple_of(me * part, part), part)] = block_ref[...]
-        for k, stage in enumerate(stages):
+        for source, target in zip(cached_refs, outs):
+            target[place] = source[...]
+        greet(stages + bits_of("seq"))
+        used = iter(range(slots))
+
+        def send(piece, stage):
+            slot = next(used)
+            return swap(piece, piece, send_sem.at[slot], recv_sem.at[slot], stage)
+
+        def tp_step(k, stage):
             wide = part << k
-            start = pl.multiple_of((me // (1 << k)) * wide, wide)
-            piece = out_ref.at[:, pl.ds(start, wide)]
-            swap(piece, piece, send_sem.at[k], recv_sem.at[k], stage).wait()
-
+            start_at = pl.multiple_of((me // (1 << k)) * wide, wide)
+            flying = []
+            return (
+                stage,
+                4.0,
+                lambda: flying.append(send(out_ref.at[:, pl.ds(start_at, wide)], stage)),
+                lambda: flying[0].wait(),
+            )
+
+        chains = [[tp_step(k, stage) for k, stage in enumerate(stages)]]
+        for target in outs:
+            def view(j, _, target=target):
+                return target.at[pl.ds((place // (1 << j)) * (1 << j), 1 << j)]
+
+            chains.append(doubling(count, [], view, send))
+        advance(chains)
+
+    shapes = [jax.ShapeDtypeStruct((rows, part * tp_count), block.dtype)]
+    for one in cached:
+        shapes.append(jax.ShapeDtypeStruct((1 << count, *one.shape), one.dtype))
     return pl.pallas_call(
         kernel,
-        out_shape=jax.ShapeDtypeStruct((rows, part * count), block.dtype),
-        in_specs=[pl.BlockSpec(memory_space=VMEM)],
-        out_specs=pl.BlockSpec(memory_space=VMEM),
-        scratch_shapes=[pltpu.SemaphoreType.DMA((len(stages),))] * 2,
+        out_shape=tuple(shapes),
+        in_specs=[pl.BlockSpec(memory_space=VMEM)] * (1 + many),
+        out_specs=tuple(pl.BlockSpec(memory_space=VMEM) for _ in shapes),
+        scratch_shapes=[pltpu.SemaphoreType.DMA((slots,))] * 2,
         compiler_params=pltpu.CompilerParams(collective_id=3, has_side_effects=True),
-        name="gather_columns",
-    )(block)
+        name="gather_front",
+    )(block, *cached)
 
 
 def sum_over_tp(block):
@@ -228,21 +259,58 @@
     return sum(bit(me, k) * (1 << (count - 1 - k)) for k in range(count))
 
 
+def carrier(stage):
+    axis, place = stage
+    return {"tp": "y", "share": "s"}.get(axis) or "cxz"[min(place, 2)]
+
+
 def advance(chains):
-    for turn in range(max(len(chain) for chain in chains)):
-        for chain in chains:
-            if turn < len(chain):
-                chain[turn]()
+    left = [sum(step[1] for step in chain) for chain in chains]
+    place, busy, events = [0] * len(chains), set(), []
+    waiting, now = set(range(len(chains))), 0.0
+    while waiting or events:
+        for c in sorted(waiting, key=lambda c: (-left[c], c)):
+            stage, cost, start, _ = chains[c][place[c]]
+            if carrier(stage) not in busy:
+                start()
+                busy.add(carrier(stage))
+                waiting.remove(c)
+                heapq.heappush(events, (now + cost, c))
+        now, c = heapq.heappop(events)
+        stage, cost, _, end = chains[c][place[c]]
+        end()
+        busy.remove(carrier(stage))
+        left[c] -= cost
+        place[c] += 1
+        if place[c] < len(chains[c]):
+            waiting.add(c)
+
+
+def doubling(count, axis_hops, view, send):
+    steps = []
+    plan = [(("seq", count - 1 - j), j, None) for j in range(count)]
+    plan[count - 1 : count - 1] = axis_hops
+    for stage, j, columns in plan:
+        flying = []
+
+        def start(stage=stage, j=j, columns=columns, flying=flying):
+            flying.append(send(view(j, columns), stage))
+
+        price = {"z": max(2.0, 1.0 * (1 << j)), "x": 1 << j, "y": 1 << j, "c": 0.3 * (1 << j)}[
+            carrier(stage)
+        ]
+        steps.append((stage, price, start, lambda flying=flying: flying[0].wait()))
+    return steps
 
 
 def spread_rows(rows, share):
     count = lax.axis_size("seq").bit_length() - 1
     blocks = 1 << count
     tall, wide = rows.shape
-    quarter = wide // 4
+    part = wide // 8
     experts = share.shape[0]
     stages = bits_of("seq") + bits_of("tp")
-    slots = 4 * count + 1
+    slots = 7 * count + 2
 
     def kernel(rows_ref, share_ref, out_ref, share_out, send_sem, recv_sem):
         place = reversed_index(count)
@@ -251,43 +319,34 @@
         share_out[place] = share_ref[...]
         greet(stages)
         used = iter(range(slots))
-        flying = {}
-
-        def hop(name, stage, view):
-            def act():
-                if name in flying:
-                    flying[name].wait()
-                slot = next(used)
-                piece = view()
-                flying[name] = swap(piece, piece, send_sem.at[slot], recv_sem.at[slot], stage)
-
-            return act
+
+        def send(piece, stage):
+            slot = next(used)
+            return swap(piece, piece, send_sem.at[slot], recv_sem.at[slot], stage)
 
         def span_of(j):
             return pl.ds((place // (1 << j)) * (1 << j), 1 << j)
 
-        def rows_view(j, start, size):
-            return lambda: out_ref.at[span_of(j), :, pl.ds(start, size)]
-
-        own = pl.multiple_of(tp * quarter, quarter)
-        crossing = [
-            hop("q", ("seq", count - 1 - j), rows_view(j, own, quarter)) for j in range(count - 1)
-        ]
-        crossing.append(hop("q", ("tp", 0), rows_view(count - 1, own, quarter)))
-        crossing.append(hop("q", ("seq", 0), rows_view(count - 1, 0, 2 * quarter)))
-        chains = [crossing]
-        for part in (2, 3):
-            chains.append([
-                hop(part, ("seq", count - 1 - j), rows_view(j, part * quarter, quarter))
-                for j in range(count)
-            ])
-        chains.append([
-            hop("s", ("seq", count - 1 - j), lambda j=j: share_out.at[span_of(j)])
-            for j in range(count)
-        ])
+        chains = []
+        for n in range(2):
+            base = 2 * n * part
+            own = pl.multiple_of(base + tp * part, part)
+
+            def view(j, columns, base=base, own=own):
+                if columns is None and j == count - 1:
+                    return out_ref.at[span_of(j), :, pl.ds(base, 2 * part)]
+                return out_ref.at[span_of(j), :, pl.ds(own, part)]
+
+            chains.append(doubling(count, [(("tp", 0), count - 1, "own")], view, send))
+        for n in range(4, 8):
+            chains.append(
+                doubling(
+                    count, [], lambda j, _, n=n: out_ref.at[span_of(j), :, pl.ds(n * part, part)], send
+                )
+            )
+        small = doubling(count, [], lambda j, _: share_out.at[span_of(j)], send)
+        chains.append([(("share", 0), cost, start, end) for _, cost, start, end in small])
         advance(chains)
-        for copy in flying.values():
-            copy.wait()
 
     return pl.pallas_call(
         kernel,
@@ -313,9 +372,25 @@
     w = half // groups
     stages = bits_of("seq") + bits_of("tp")
     slots = groups * (2 * count + 1)
+    keys, scratch = [], []
+
+    def reserve(key, *shape):
+        keys.append(key)
+        scratch.append(VMEM((*shape, tall, w), jnp.bfloat16))
+
+    for g in range(groups):
+        wide_at = 1 if g < groups // 2 else count
+        for j in range(count):
+            copies = 2 if j < wide_at else 1
+            for h in range(copies):
+                reserve(("got", g, j, h), blocks >> (j + 1))
+            reserve(("sum", g, j), copies, blocks >> (j + 1))
+        reserve(("got", g, "tp"), blocks >> wide_at)
+        reserve(("sum", g, "tp"), 1, blocks >> wide_at)
 
     def kernel(part_ref, out_ref, *rest):
-        buffers, (send_sem, recv_sem) = iter(rest[:-2]), rest[-2:]
+        buffers = dict(zip(keys, rest[:-2]))
+        send_sem, recv_sem = rest[-2:]
         greet(stages)
         me, tp = lax.axis_index("seq"), lax.axis_index("tp")
         used = iter(range(slots))
@@ -332,121 +407,64 @@
 
             lax.fori_loop(0, size, body, 0)
 
-        def scatter(state, j):
-            size = 1 << (count - 1 - j)
-            got, out = next(buffers), next(buffers)
-            mine = bit(me, j)
-            source = state
-            copy = send(source.at[pl.ds((1 - mine) * size, size)], got, ("seq", j))
-
-            def end():
-                copy.wait()
-                add(size, source, mine * size, got, out)
-                return out
-
-            return end
-
-        def straight(group):
-            ends, states = {}, {}
-            views = [part_ref.at[:, :, pl.ds(h * half + group * w, w)] for h in range(2)]
-
-            def step(j):
-                def act():
-                    for h in range(2):
-                        state = views[h] if j == 0 else ends[h]()
-                        ends[h] = scatter(state, j)
-
-                return act
-
-            def cross():
-                both, got = next(buffers), next(buffers)
-                for h in range(2):
-                    both[h] = ends[h]()[0]
-                states["both"], states["got"] = both, got
-                states["copy"] = send(both.at[1 - tp], got, ("tp", 0))
-
-            def finish():
-                states["copy"].wait()
-                out_ref[:, group * w : (group + 1) * w] = states["both"][tp].astype(
-                    jnp.float32
-                ) + states["got"][...].astype(jnp.float32)
-
-            return [step(j) for j in range(count)] + [cross, finish]
-
-        def crossing(group):
-            ends, states = {}, {}
-            size = blocks // 2
-
-            def first():
-                for h in range(2):
-                    got = next(buffers)
-                    mine = bit(me, 0)
-                    view = part_ref.at[:, :, pl.ds(h * half + group * w, w)]
-                    copy = send(view.at[pl.ds((1 - mine) * size, size)], got, ("seq", 0))
-                    states[h] = (view, mine, got, copy)
-                states["both"] = next(buffers)
-
-            def cross():
-                both, got = states["both"], next(buffers)
-                for h in range(2):
-                    view, mine, landed, copy = states[h]
-                    copy.wait()
-                    add(size, view, mine * size, landed, both.at[h])
-                states["got"] = got
-                states["copy"] = send(both.at[1 - tp], got, ("tp", 0))
-
-            def second():
-                states["copy"].wait()
-                out = next(buffers)
-                add(size, states["both"].at[tp], 0, states["got"], out)
-                ends[0] = scatter(out, 1)
-
-            def step(j):
-                def act():
-                    ends[0] = scatter(ends[0](), j)
-
-                return act
-
-            def finish():
-                out_ref[:, group * w : (group + 1) * w] = ends[0]()[0].astype(jnp.float32)
-
-            return [first, cross, second] + [step(j) for j in range(2, count)] + [finish]
-
-        advance([crossing(g) if g < groups // 2 else straight(g) for g in range(groups)])
-
-    def shapes():
-        bf16 = jnp.bfloat16
-        listing = []
-
-        def scatter(j):
-            size = 1 << (count - 1 - j)
-            listing.extend([VMEM((size, tall, w), bf16)] * 2)
-
-        def straight():
-            cross = [VMEM((2, tall, w), bf16), VMEM((tall, w), bf16)]
-            return [lambda j=j: (scatter(j), scatter(j)) for j in range(count)] + [
-                lambda: listing.extend(cross), lambda: None
-            ]
-
-        def crossing():
-            size = blocks // 2
-            block = VMEM((size, tall, w), bf16)
-            pair = VMEM((2, size, tall, w), bf16)
-            return [
-                lambda: listing.extend([block, block, pair]),
-                lambda: listing.extend([block]),
-                lambda: (listing.extend([block]), scatter(1)),
-            ] + [lambda j=j: scatter(j) for j in range(2, count)] + [lambda: None]
-
-        advance([crossing() if g < groups // 2 else straight() for g in range(groups)])
-        return listing
+        def chain(g):
+            wide_at = 1 if g < groups // 2 else count
+            state = {
+                "views": [part_ref.at[:, :, pl.ds(h * half + g * w, w)] for h in range(2)]
+            }
+
+            def seq_step(j, copies):
+                size = blocks >> (j + 1)
+                mine = bit(me, j)
+                copying = []
+
+                def start():
+                    for h in range(copies):
+                        away = state["views"][h].at[pl.ds((1 - mine) * size, size)]
+                        copying.append(send(away, buffers["got", g, j, h], ("seq", j)))
+
+                def end():
+                    out = buffers["sum", g, j]
+                    for h in range(copies):
+                        copying[h].wait()
+                        add(size, state["views"][h], mine * size, buffers["got", g, j, h], out.at[h])
+                    state["both"] = out
+                    state["views"] = [out.at[h] for h in range(copies)]
+
+                price = {"z": 1.0 * size, "x": size, "c": 0.3 * size}[carrier(("seq", j))]
+                return (("seq", j), max(2.0, price) * copies, start, end)
+
+            def tp_step():
+                size = blocks >> wide_at
+                copying = []
+
+                def start():
+                    away = state["both"].at[1 - tp]
+                    copying.append(send(away, buffers["got", g, "tp"], ("tp", 0)))
+
+                def end():
+                    copying[0].wait()
+                    out = buffers["sum", g, "tp"]
+                    add(size, state["both"].at[tp], 0, buffers["got", g, "tp"], out.at[0])
+                    state["views"] = [out.at[0]]
+
+                return (("tp", 0), size, start, end)
+
+            steps = [seq_step(j, 2 if j < wide_at else 1) for j in range(count)]
+            steps.insert(wide_at, tp_step())
+            return steps, state
+
+        made = [chain(g) for g in range(groups)]
+        advance([steps for steps, _ in made])
+        for g, (_, state) in enumerate(made):
+            out_ref[:, g * w : (g + 1) * w] = state["views"][0][0].astype(jnp.float32)
 
     return pl.pallas_call(
         kernel,
         out_shape=jax.ShapeDtypeStruct((tall, half), jnp.float32),
         in_specs=[pl.BlockSpec(memory_space=VMEM)],
         out_specs=pl.BlockSpec(memory_space=VMEM),
-        scratch_shapes=shapes()
+        scratch_shapes=scratch
         + [pltpu.SemaphoreType.DMA((slots,)), pltpu.SemaphoreType.DMA((slots,))],
         compiler_params=pltpu.CompilerParams(
             collective_id=6, has_side_effects=True, vmem_limit_bytes=56 << 20
@@ -534,7 +552,7 @@
     width_part = tokens.shape[1]
     shard_rows = prefix_keys.shape[0]
     prefix_length = shard_rows * seq_count // 2
-    full_x = gather_columns(tokens)
+    full_x, cached_k, cached_v = gather_front(tokens, prefix_keys, prefix_values)
     width = full_x.shape[1]
     normed = normalize(full_x.astype(f32), attn_gain).astype(bf16)
     heads = w_query.shape[1] // HD
@@ -554,12 +572,13 @@
     key_rows = key_rows.reshape(tok_dev, heads * HD)
     value_rows = jnp.dot(normed, w_value, preferred_element_type=f32).astype(bf16)
     pieces = (
-        lax.all_gather(prefix_keys, "seq", axis=0, tiled=True),
-        lax.all_gather(prefix_values, "seq", axis=0, tiled=True),
+        cached_k.reshape(-1, heads * HD),
+        cached_v.reshape(-1, heads * HD),
     )
     count = pieces[0].shape[0]
     shard_ids = jnp.arange(count) // shard_rows
-    key_group = lookup(shard_ids, shard_group)
+    bits = seq_count.bit_length() - 1
+    key_group = lookup(shard_ids, shard_group.reshape((2,) * bits).transpose().reshape(-1))
     fold_allowed = own_group[:, None] == key_group[None, :]
     own_allowed = (own_request[:, None] == own_request[None, :]) & (
         local_index[None, :] <= local_index[:, None]

time: 326 us -> 316 us (0.969)
  Pallas kernels: 204 us -> 240 us
  waiting for transfers between devices: 38.1 us -> 4.18 us
  between operations: 14.5 us -> 1.06 us
    all_gather x2 -> x0, waiting for transfers between devices: 35.9 us -> none  [the longest x1 35.9 us: on_device(): lax.all_gather(prefix_values, 'seq', axis=0, tiled=True)]
    pallas_call x1, Pallas kernels: 11.1 us -> 34.9 us  [gather_front(): pl.pallas_call(kernel, out_shape=tuple(shapes), in_specs=[pl.BlockSpec(me...]
    pallas_call x1, Pallas kernels: 66.5 us -> 79.1 us  [spread_rows(): pl.pallas_call(kernel, out_shape=(jax.ShapeDtypeStruct((blocks, tall, wid...]
  transfers between devices with their start and end apart: 6 -> 4, of which waited for: 2 -> 1; matrix products, arithmetic and copies ran while one was open for 7% -> 4% of each run, Pallas kernels for 3% -> 0%
where the time goes in v4:
time: 316 us; the launch traced here: 315 us
  Pallas kernels  240 us (76%)
  matrix products  31.4 us (10%)
  other arithmetic  20 us (6%)
  starting transfers between devices  12 us (4%)
  local copies, waits for them, and re-layouts  6.42 us (2%)
  waiting for transfers between devices  4.18 us (1%)
    pallas_call x1, Pallas kernels, spread_rows(): pl.pallas_call(kernel, out_shape=(jax.ShapeDtypeStruct((blocks, tall, wid...  79.1 us
    pallas_call x1, Pallas kernels, collect_rows(): pl.pallas_call(kernel, out_shape=jax.ShapeDtypeStruct((tall, half), jnp.f...  68 us
    pallas_call x1, Pallas kernels, gather_front(): pl.pallas_call(kernel, out_shape=tuple(shapes), in_specs=[pl.BlockSpec(me...  34.9 us
    pallas_call x1, Pallas kernels, last_rows(): pl.pallas_call(kernel, out_shape=jax.ShapeDtypeStruct((rows, part), jnp.b...  16.6 us
    pallas_call x1, Pallas kernels, sum_over_tp(): pl.pallas_call(kernel, out_shape=jax.ShapeDtypeStruct((rows, part), jnp.f...  16.5 us
    pallas_call x1, Pallas kernels, log_softmax(): pl.pallas_call(kernel, out_shape=jax.ShapeDtypeStruct((rows, part), jnp.f...  16.3 us
    ppermute x4, starting transfers between devices, from_behind(): lax.ppermute(value, axis, [(source, source + steps) for source in range(l...  12 us
    pallas_call x1, Pallas kernels, attention(): pl.pallas_call(kernel, out_shape=jax.ShapeDtypeStruct((tall, wide), jnp.b...  8.97 us
  transfers between devices with their start and end apart: 4, of which 1 were waited for; matrix products, arithmetic and copies ran while one was open for 4% of the time, Pallas kernels for 0%

profile of v4, /device:TPU:0, one launch (start us, length us, event | category | flops | bytes accessed | tf_op | source)
XLA Modules:
  0.0 315.4 jit_solution(1351860326842339614)
XLA Ops:
  0.7 1.0 reduce-window.7
  1.7 1.2 broadcast_add_fusion
  2.9 0.7 convert_reduce_fusion
  3.6 1.3 select_reduce_fusion.2
  4.8 0.7 convert_element_type.82
  5.5 34.9 %gather_front.1 = (bf16[128,2048]{1,0:T(8,128)(2,1)}, bf16[16,32,1024]{2,1,0:T(8,128)(2,1)}, bf16[16,32,1024]{2,1,0:T(8,128)(2,1)}) custom-call(bf16[128,1024]{1,0:T(8,128)(2,1)} %block_ref.1, bf16[32,1024]{1,0:T(8,128)(2,1)} %rest_0_.1, bf16[32,1024]{1,0:T(8,128)(2,1)} %rest_1_.1), custom_call_target="tpu_custom_call" | custom-call | tf_op jit(solution)/shard_map/gather_front/pallas_call | solution.py:210
  40.4 1.4 fusion.7
  41.8 3.3 %convolution_convert_fusion.1 = bf16[128,1024]{1,0:T(8,128)(2,1)S(1)} fusion(bf16[2048,1024]{1,0:T(8,128)(2,1)} %param.23, bf16[128,2048]{1,0:T(8,128)(2,1)} %get-tuple-element.7, f32[2048]{0:T(1024)S(1)} %convert_element_type.82, f32[128]{0:T(128)S(1)} %add_rsqrt_fusion.1), kind=kOutput, calls=%fused_computation.14 | convolution fusion | flops 538050560 | bytes 4989440 | tf_op jit(solution)/shard_map/dot_general | solution.py:573
  45.1 0.8 convolution_bitcast_fusion
  46.0 1.3 copy-done.4
  47.3 0.8 convolution_bitcast_fusion.1
  48.2 0.3 multiply_cosine_fusion
  48.5 1.2 subtract_convert_fusion
  50.0 2.1 collective-permute-start.3
  52.1 5.2 %collective-permute-start.2 = (bf16[128,2048]{1,0:T(8,128)(2,1)S(1)}, bf16[128,2048]{1,0:T(8,128)(2,1)}, u32[]{:S(2)}, u32[]{:S(2)}) collective-permute-start(bf16[128,2048]{1,0:T(8,128)(2,1)S(1)} %pad_maximum_fusion.rest_0_.rest_5_), channel_id=1, source_target_pairs={{0,6},{2,8},{4,10},{6,12},{8,14},{10,16},{12,18},{14,20},{16,22},{... | collective-permute-start | bytes 1572872 | tf_op jit(solution)/shard_map/ppermute | solution.py:21
  57.2 2.1 collective-permute-start.1
  59.3 2.6 collective-permute-start
  61.9 0.5 broadcast_compare_fusion.2
  62.5 0.6 broadcast_compare_fusion
  63.4 0.7 compare_dynamic-update-slice_fusion
  64.2 0.8 and_dynamic-update-slice_fusion.4
  65.0 0.8 and_dynamic-update-slice_fusion.3
  65.7 0.7 and_dynamic-update-slice_fusion.2
  66.5 0.8 and_dynamic-update-slice_fusion.1
  67.2 0.8 and_dynamic-update-slice_fusion
  68.0 1.8 pad_maximum_fusion.1
  69.8 1.3 reshape.217.gain_ref
  71.1 0.7 convert_element_type.98
  71.8 1.7 copy.32
  73.5 0.9 broadcast_select_fusion.bias_ref
  74.4 4.2 %collective-permute-done.1.rest_2_.rest_7_ = bf16[128,2048]{1,0:T(8,128)(2,1)} collective-permute-done((bf16[128,2048]{1,0:T(8,128)(2,1)S(1)}, bf16[128,2048]{1,0:T(8,128)(2,1)}, u32[]{:S(2)}, u32[]{:S(2)}) %collective-permute-start.1) | collective-permute-done | bytes 524320 | tf_op jit(solution)/shard_map/ppermute | solution.py:21
  78.6 9.0 %attention.1 = bf16[128,1024]{1,0:T(8,128)(2,1)} custom-call(bf16[128,1024]{1,0:T(8,128)(2,1)} %bitcast.53, bf16[512,1024]{1,0:T(8,128)(2,1)} %bitcast.57, bf16[512,1024]{1,0:T(8,128)(2,1)} %bitcast.58, f32[128,1152]{1,0:T(8,128)} %broadcast_select_fusion.bias_ref, bf16[128,2048]{1,0:T(8,128)(2,1)} %copy-done.2, ...), custom_call_target="tpu_custom_call" | custom-call | flops 603979776 | bytes 4718592 | tf_op jit(solution)/shard_map/attention/pallas_call | solution.py:508
  87.6 3.8 %convolution_convert_fusion.block_ref = bf16[128,2048]{1,0:T(8,128)(2,1)} fusion(bf16[128,1024]{1,0:T(8,128)(2,1)} %attention.1, bf16[1024,2048]{1,0:T(8,128)(2,1)} %param.24), kind=kOutput, calls=%fused_computation.2 | convolution fusion | flops 537133056 | bytes 4980736 | tf_op jit(solution)/shard_map/dot_general | solution.py:597
  91.4 16.5 %sum_over_tp.1 = f32[128,2048]{1,0:T(8,128)} custom-call(bf16[128,2048]{1,0:T(8,128)(2,1)} %convolution_convert_fusion.block_ref), custom_call_target="tpu_custom_call" | custom-call | tf_op jit(solution)/shard_map/sum_over_tp/pallas_call | solution.py:237
  107.9 1.6 fusion.4
  109.5 0.2 fusion.6.rows_ref
  109.7 0.3 fusion.24
  110.1 79.1 %spread_rows.1 = (bf16[16,128,2048]{2,1,0:T(8,128)(2,1)S(1)}, f32[16,16,128]{2,1,0:T(8,128)S(1)}) custom-call(bf16[128,2048]{1,0:T(8,128)(2,1)S(1)} %fusion.6.rows_ref, f32[16,128]{1,0:T(8,128)S(1)} %bitcast.47), custom_call_target="tpu_custom_call" | custom-call | tf_op jit(solution)/shard_map/spread_rows/pallas_call | solution.py:351
  189.2 4.5 %fusion.2 = f32[2048,512]{1,0:T(8,128)S(1)} fusion(bf16[2048,2048]{1,0:T(8,128)(2,1)S(1)} %bitcast.48, bf16[1,2048,512]{2,1,0:T(8,128)(2,1)S(1)} %copy-done.13), kind=kOutput, calls=%fused_computation.5 | convolution fusion | flops 4294967296 | bytes 14680064 | tf_op jit(solution)/shard_map/dot_general | solution.py:610
  193.7 5.1 %multiply_convert_fusion.1 = bf16[2048,512]{1,0:T(8,128)(2,1)S(1)} fusion(f32[2048,512]{1,0:T(8,128)S(1)} %fusion.2, bf16[2048,2048]{1,0:T(8,128)(2,1)S(1)} %bitcast.49, bf16[1,2048,512]{2,1,0:T(8,128)(2,1)S(1)} %copy-done.14), kind=kOutput, calls=%fused_computation.1 | convolution fusion | flops 4301258752 | bytes 16777216 | tf_op jit(solution)/shard_map/dot_general | solution.py:611
  198.9 6.8 %multiply_convert_fusion = bf16[2048,2048]{1,0:T(8,128)(2,1)} fusion(bf16[2048,512]{1,0:T(8,128)(2,1)S(1)} %multiply_convert_fusion.1, f32[2048]{0:T(1024)S(1)} %bitcast.60, bf16[1,512,2048]{2,1,0:T(8,128)(2,1)S(1)} %copy-done), kind=kOutput, calls=%fused_computation | convolution fusion | flops 4303355904 | bytes 12591104 | tf_op jit(solution)/shard_map/dot_general | solution.py:613
  205.7 68.0 %collect_rows.1 = f32[128,1024]{1,0:T(8,128)} custom-call(bf16[16,128,2048]{2,1,0:T(8,128)(2,1)} %bitcast.50), custom_call_target="tpu_custom_call" | custom-call | tf_op jit(solution)/shard_map/collect_rows/pallas_call | solution.py:462
  273.7 1.1 add_convert_fusion
  274.8 0.8 fusion.13.chosen_ref
  275.7 16.6 %last_rows.1 = bf16[8,1024]{1,0:T(8,128)(2,1)} custom-call(f32[8,1024]{1,0:T(8,128)} %fusion.13.chosen_ref, bf16[1,1024]{1,0:T(2,128)(2,1)} %reshape.217.gain_ref), custom_call_target="tpu_custom_call" | custom-call | tf_op jit(solution)/shard_map/last_rows/pallas_call | solution.py:99
  292.3 5.3 %fusion.25.logits_ref = f32[8,3144]{1,0:T(8,128)} fusion(bf16[8,1024]{1,0:T(8,128)(2,1)} %last_rows.1, bf16[1024,3144]{0,1:T(8,128)(2,1)} %param.37), kind=kOutput, calls=%fused_computation.84 | convolution fusion | flops 51511296 | bytes 6555904 | tf_op jit(solution)/shard_map/dot_general | solution.py:647
  297.5 16.3 %log_softmax.1 = f32[8,3144]{1,0:T(8,128)} custom-call(f32[8,3144]{1,0:T(8,128)} %fusion.25.logits_ref), custom_call_target="tpu_custom_call" | custom-call | tf_op jit(solution)/shard_map/log_softmax/pallas_call | solution.py:147
  313.9 1.5 copy.39
  (53 shorter events, 1.0 us)
Async XLA Ops:
  0.6 198.3 %copy-start = (bf16[1,512,2048]{2,1,0:T(8,128)(2,1)S(1)}, bf16[1,512,2048]{2,1,0:T(8,128)(2,1)}, u32[]{:S(2)}) copy-start(bf16[1,512,2048]{2,1,0:T(8,128)(2,1)} %param.34) | copy-start | bytes 6291460
  0.7 4.9 %copy-start.8 = (s32[128]{0:T(128)}, s32[128]{0:T(128)S(1)}, u32[]{:S(2)}) copy-start(s32[128]{0:T(128)S(1)} %iota_add_fusion.4) | copy-start | bytes 1540
  3.6 1.3 copy-start.7
  40.4 4.7 %copy-start.1 = (bf16[128,2048]{1,0:T(8,128)(2,1)S(1)}, bf16[128,2048]{1,0:T(8,128)(2,1)}, u32[]{:S(2)}) copy-start(bf16[128,2048]{1,0:T(8,128)(2,1)} %get-tuple-element.7) | copy-start | bytes 1572868
  40.4 4.7 %copy-start.3 = (bf16[2048,1024]{1,0:T(8,128)(2,1)S(1)}, bf16[2048,1024]{1,0:T(8,128)(2,1)}, u32[]{:S(2)}) copy-start(bf16[2048,1024]{1,0:T(8,128)(2,1)} %param.22) | copy-start | bytes 12582916
  45.1 2.2 copy-start.4
  48.1 14.9 %copy-start.12 = (s32[16]{0:T(128)S(1)}, s32[16]{0:T(128)}, u32[]{:S(2)}) copy-start(s32[16]{0:T(128)} %param.27) | copy-start | bytes 196
  49.9 28.6 %copy-start.2 = (bf16[128,2048]{1,0:T(8,128)(2,1)}, bf16[128,2048]{1,0:T(8,128)(2,1)S(1)}, u32[]{:S(2)}) copy-start(bf16[128,2048]{1,0:T(8,128)(2,1)S(1)} %pad_maximum_fusion.rest_0_.rest_5_) | copy-start | bytes 1572868
  50.0 24.4 %collective-permute-start.3 = (bf16[128,2048]{1,0:T(8,128)(2,1)S(1)}, bf16[128,2048]{1,0:T(8,128)(2,1)}, u32[]{:S(2)}, u32[]{:S(2)}) collective-permute-start(bf16[128,2048]{1,0:T(8,128)(2,1)S(1)} %pad_maximum_fusion.rest_0_.rest_5_), channel_id=1, source_target_pairs={{0,8},{2,10},{4,12},{6,14},{8,16},{10,18},{12,20},{14,22},{16,24},... | collective-permute-start | bytes 1572872 | tf_op jit(solution)/shard_map/ppermute | solution.py:21
  52.1 22.3 %collective-permute-start.2 = (bf16[128,2048]{1,0:T(8,128)(2,1)S(1)}, bf16[128,2048]{1,0:T(8,128)(2,1)}, u32[]{:S(2)}, u32[]{:S(2)}) collective-permute-start(bf16[128,2048]{1,0:T(8,128)(2,1)S(1)} %pad_maximum_fusion.rest_0_.rest_5_), channel_id=1, source_target_pairs={{0,6},{2,8},{4,10},{6,12},{8,14},{10,16},{12,18},{14,20},{16,22},{... | collective-permute-start | bytes 1572872 | tf_op jit(solution)/shard_map/ppermute | solution.py:21
  57.2 21.3 %collective-permute-start.1 = (bf16[128,2048]{1,0:T(8,128)(2,1)S(1)}, bf16[128,2048]{1,0:T(8,128)(2,1)}, u32[]{:S(2)}, u32[]{:S(2)}) collective-permute-start(bf16[128,2048]{1,0:T(8,128)(2,1)S(1)} %pad_maximum_fusion.rest_0_.rest_5_), channel_id=1, source_target_pairs={{0,4},{2,6},{4,8},{6,10},{8,12},{10,14},{12,16},{14,18},{16,20},{1... | collective-permute-start | bytes 1572872 | tf_op jit(solution)/shard_map/ppermute | solution.py:21
  59.3 19.2 %collective-permute-start = (bf16[128,2048]{1,0:T(8,128)(2,1)S(1)}, bf16[128,2048]{1,0:T(8,128)(2,1)}, u32[]{:S(2)}, u32[]{:S(2)}) collective-permute-start(bf16[128,2048]{1,0:T(8,128)(2,1)S(1)} %pad_maximum_fusion.rest_0_.rest_5_), channel_id=1, source_target_pairs={{0,2},{2,4},{4,6},{6,8},{8,10},{10,12},{12,14},{14,16},{16,18},{18... | collective-permute-start | bytes 1572872 | tf_op jit(solution)/shard_map/ppermute | solution.py:21
  87.5 22.2 %copy-start.6 = (bf16[2048,16]{0,1:T(8,128)(2,1)S(1)}, bf16[2048,16]{0,1:T(8,128)(2,1)}, u32[]{:S(2)}) copy-start(bf16[2048,16]{0,1:T(8,128)(2,1)} %param.31) | copy-start | bytes 196612
  87.5 22.5 %copy-start.10 = (s32[128,8]{0,1:T(8,128)S(1)}, s32[128,8]{0,1:T(8,128)}, u32[]{:S(2)}) copy-start(s32[128,8]{0,1:T(8,128)} %param.35) | copy-start | bytes 12292
  107.9 81.3 %copy-start.13 = (bf16[1,2048,512]{2,1,0:T(8,128)(2,1)S(1)}, bf16[1,2048,512]{2,1,0:T(8,128)(2,1)}, u32[]{:S(2)}) copy-start(bf16[1,2048,512]{2,1,0:T(8,128)(2,1)} %param.32) | copy-start | bytes 6291460
  189.2 4.5 %copy-start.14 = (bf16[1,2048,512]{2,1,0:T(8,128)(2,1)S(1)}, bf16[1,2048,512]{2,1,0:T(8,128)(2,1)}, u32[]{:S(2)}) copy-start(bf16[1,2048,512]{2,1,0:T(8,128)(2,1)} %param.33) | copy-start | bytes 6291460
  205.7 69.1 %copy-start.9 = (s32[128]{0:T(128)S(1)}, s32[128]{0:T(128)}, u32[]{:S(2)}) copy-start(s32[128]{0:T(128)} %copy-done.8) | copy-start | bytes 1540
  205.7 69.2 %copy-start.11 = (s32[8]{0:T(128)S(1)}, s32[8]{0:T(128)}, u32[]{:S(2)}) copy-start(s32[8]{0:T(128)} %get-tuple-element.29) | copy-start | bytes 100
  274.8 40.6 %copy-start.5 = (bf16[128,1024]{1,0:T(8,128)(2,1)}, bf16[128,1024]{1,0:T(8,128)(2,1)S(1)}, u32[]{:S(2)}) copy-start(bf16[128,1024]{1,0:T(8,128)(2,1)S(1)} %add_convert_fusion) | copy-start | bytes 786436

commit v5 on v4

--- a/solution.py
+++ b/solution.py
@@ -73,93 +73,82 @@
     return [(axis, bit) for bit in range(lax.axis_size(axis).bit_length() - 1)]
 
 
-def last_rows(chosen, gain, width):
+def head_tail(chosen, gain, w_head, width):
     seq_stages, tp_stages = bits_of("seq"), bits_of("tp")
     stages = seq_stages + tp_stages
     rows, part = chosen.shape
-
-    def kernel(chosen_ref, gain_ref, out_ref, held, got, sq_held, sq_got, send_sem, recv_sem):
+    vocab = w_head.shape[1]
+    ns, nt = len(seq_stages), len(tp_stages)
+
+    def kernel(chosen_ref, gain_ref, head_hbm, out_ref, head, rows_held, rows_got, sq_held, sq_got,
+               lg_held, lg_got, st_held, st_got, head_sem, send_sem, recv_sem):
+        loading = pltpu.make_async_copy(head_hbm, head, head_sem)
+        loading.start()
         greet(stages)
-        held[0] = chosen_ref[...]
-        count = len(seq_stages)
+        used = iter(range(2 * ns + 2 * nt))
+
+        def exchange(held, got, k, stage):
+            n = next(used)
+            swap(held.at[k], got.at[k], send_sem.at[n], recv_sem.at[n], stage).wait()
+
+        rows_held[0] = chosen_ref[...]
         for k, stage in enumerate(seq_stages):
-            swap(held.at[k], got.at[k], send_sem.at[k], recv_sem.at[k], stage).wait()
-            held[k + 1] = held[k] + got[k]
-        total = held[count]
-        sq_held[0] = jnp.broadcast_to(jnp.sum(total * total, -1, keepdims=True), (rows, 128))
+            exchange(rows_held, rows_got, k, stage)
+            rows_held[k + 1] = rows_held[k] + rows_got[k]
+        last = rows_held[ns]
+        sq_held[0] = jnp.broadcast_to(jnp.sum(last * last, -1, keepdims=True), (rows, 128))
         for k, stage in enumerate(tp_stages):
-            n = count + k
-            swap(sq_held.at[k], sq_got.at[k], send_sem.at[n], recv_sem.at[n], stage).wait()
+            exchange(sq_held, sq_got, k, stage)
             sq_held[k + 1] = sq_held[k] + sq_got[k]
-        square = sq_held[len(tp_stages)][:, :1]
-        scaled = total * lax.rsqrt(square / width + EPS) * gain_ref[...].astype(jnp.float32)
-        out_ref[...] = scaled.astype(jnp.bfloat16)
-
-    ns, nt = len(seq_stages), len(tp_stages)
-    return pl.pallas_call(
-        kernel,
-        out_shape=jax.ShapeDtypeStruct((rows, part), jnp.bfloat16),
-        in_specs=[pl.BlockSpec(memory_space=VMEM)] * 2,
-        out_specs=pl.BlockSpec(memory_space=VMEM),
-        scratch_shapes=[
-            VMEM((ns + 1, rows, part), jnp.float32),
-            VMEM((ns, rows, part), jnp.float32),
-            VMEM((nt + 1, rows, 128), jnp.float32),
-            VMEM((nt, rows, 128), jnp.float32),
-            pltpu.SemaphoreType.DMA((ns + nt,)),
-            pltpu.SemaphoreType.DMA((ns + nt,)),
-        ],
-        compiler_params=pltpu.CompilerParams(collective_id=1, has_side_effects=True),
-        name="last_rows",
-    )(chosen, gain.reshape(1, part))
-
-
-def log_softmax(logits):
-    seq_stages, tp_stages = bits_of("seq"), bits_of("tp")
-    stages = tp_stages + seq_stages
-    rows, part = logits.shape
-
-    def kernel(logits_ref, out_ref, held, got, st_held, st_got, send_sem, recv_sem):
-        greet(stages)
-        held[0] = logits_ref[...]
-        count = len(tp_stages)
+        square = sq_held[nt][:, :1]
+        final = last * lax.rsqrt(square / width + EPS) * gain_ref[...].astype(jnp.float32)
+        final = final.astype(jnp.bfloat16)
+        loading.wait()
+        lg_held[0] = jnp.dot(final, head[...], preferred_element_type=jnp.float32)
         for k, stage in enumerate(tp_stages):
-            swap(held.at[k], got.at[k], send_sem.at[k], recv_sem.at[k], stage).wait()
-            held[k + 1] = held[k] + got[k]
-        total = held[count]
-        peak = jnp.max(total, -1, keepdims=True)
-        mass = jnp.sum(jnp.exp(total - peak), -1, keepdims=True)
+            exchange(lg_held, lg_got, k, stage)
+            lg_held[k + 1] = lg_held[k] + lg_got[k]
+        logits = lg_held[nt]
+        peak = jnp.max(logits, -1, keepdims=True)
+        mass = jnp.sum(jnp.exp(logits - peak), -1, keepdims=True)
         st_held[0, :, :128] = jnp.broadcast_to(peak, (rows, 128))
         st_held[0, :, 128:] = jnp.broadcast_to(mass, (rows, 128))
         for k, stage in enumerate(seq_stages):
-            n = count + k
-            swap(st_held.at[k], st_got.at[k], send_sem.at[n], recv_sem.at[n], stage).wait()
+            exchange(st_held, st_got, k, stage)
             mine, theirs = st_held[k, :, :128], st_got[k, :, :128]
             top = jnp.maximum(mine, theirs)
             st_held[k + 1, :, :128] = top
             st_held[k + 1, :, 128:] = st_held[k, :, 128:] * jnp.exp(mine - top) + st_got[
                 k, :, 128:
             ] * jnp.exp(theirs - top)
-        last = len(seq_stages)
-        out_ref[...] = total - st_held[last, :, :1] - jnp.log(st_held[last, :, 128:129])
-
-    ns, nt = len(seq_stages), len(tp_stages)
+        out_ref[...] = logits - st_held[ns, :, :1] - jnp.log(st_held[ns, :, 128:129])
+
+    f32 = jnp.float32
+    slots = 2 * ns + 2 * nt
     return pl.pallas_call(
         kernel,
-        out_shape=jax.ShapeDtypeStruct((rows, part), jnp.float32),
-        in_specs=[pl.BlockSpec(memory_space=VMEM)],
+        out_shape=jax.ShapeDtypeStruct((rows, vocab), f32),
+        in_specs=[pl.BlockSpec(memory_space=VMEM)] * 2 + [pl.BlockSpec(memory_space=pl.ANY)],
         out_specs=pl.BlockSpec(memory_space=VMEM),
         scratch_shapes=[
-            VMEM((nt + 1, rows, part), jnp.float32),
-            VMEM((nt, rows, part), jnp.float32),
-            VMEM((ns + 1, rows, 256), jnp.float32),
-            VMEM((ns, rows, 256), jnp.float32),
-            pltpu.SemaphoreType.DMA((ns + nt,)),
-            pltpu.SemaphoreType.DMA((ns + nt,)),
+            VMEM(w_head.shape, w_head.dtype),
+            VMEM((ns + 1, rows, part), f32),
+            VMEM((ns, rows, part), f32),
+            VMEM((nt + 1, rows, 128), f32),
+            VMEM((nt, rows, 128), f32),
+            VMEM((nt + 1, rows, vocab), f32),
+            VMEM((nt, rows, vocab), f32),
+            VMEM((ns + 1, rows, 256), f32),
+            VMEM((ns, rows, 256), f32),
+            pltpu.SemaphoreType.DMA,
+            pltpu.SemaphoreType.DMA((slots,)),
+            pltpu.SemaphoreType.DMA((slots,)),
         ],
-        compiler_params=pltpu.CompilerParams(collective_id=2, has_side_effects=True),
-        name="log_softmax",
-    )(logits)
+        compiler_params=pltpu.CompilerParams(
+            collective_id=1, has_side_effects=True, vmem_limit_bytes=40 << 20
+        ),
+        name="head_tail",
+    )(chosen, gain.reshape(1, part), w_head)
 
 
 def gather_front(block, *cached):
@@ -261,7 +250,7 @@
 
 def carrier(stage):
     axis, place = stage
-    return {"tp": "y", "share": "s"}.get(axis) or "cxz"[min(place, 2)]
+    return "y" if axis == "tp" else "cxz"[min(place, 2)]
 
 
 def advance(chains):
@@ -273,13 +262,14 @@
             stage, cost, start, _ = chains[c][place[c]]
             if carrier(stage) not in busy:
                 start()
-                busy.add(carrier(stage))
+                if carrier(stage) != "c":
+                    busy.add(carrier(stage))
                 waiting.remove(c)
                 heapq.heappush(events, (now + cost, c))
         now, c = heapq.heappop(events)
         stage, cost, _, end = chains[c][place[c]]
         end()
-        busy.remove(carrier(stage))
+        busy.discard(carrier(stage))
         left[c] -= cost
         place[c] += 1
         if place[c] < len(chains[c]):
@@ -296,21 +286,28 @@
         def start(stage=stage, j=j, columns=columns, flying=flying):
             flying.append(send(view(j, columns), stage))
 
-        price = {"z": max(2.0, 1.0 * (1 << j)), "x": 1 << j, "y": 1 << j, "c": 0.3 * (1 << j)}[
+        price = {"z": max(2.0, 1.0 * (1 << j)), "x": 1 << j, "y": 1 << j, "c": 0.1 * (1 << j)}[
             carrier(stage)
         ]
         steps.append((stage, price, start, lambda flying=flying: flying[0].wait()))
     return steps
 
 
+def take_turns(chains):
+    for turn in range(max(len(chain) for chain in chains)):
+        for chain in chains:
+            if turn < len(chain):
+                chain[turn]()
+
+
 def spread_rows(rows, share):
     count = lax.axis_size("seq").bit_length() - 1
     blocks = 1 << count
     tall, wide = rows.shape
-    part = wide // 8
+    quarter = wide // 4
     experts = share.shape[0]
     stages = bits_of("seq") + bits_of("tp")
-    slots = 7 * count + 2
+    slots = 4 * count + 1
 
     def kernel(rows_ref, share_ref, out_ref, share_out, send_sem, recv_sem):
         place = reversed_index(count)
@@ -319,34 +316,43 @@
         share_out[place] = share_ref[...]
         greet(stages)
         used = iter(range(slots))
-
-        def send(piece, stage):
-            slot = next(used)
-            return swap(piece, piece, send_sem.at[slot], recv_sem.at[slot], stage)
+        flying = {}
+
+        def hop(name, stage, view):
+            def act():
+                if name in flying:
+                    flying[name].wait()
+                slot = next(used)
+                piece = view()
+                flying[name] = swap(piece, piece, send_sem.at[slot], recv_sem.at[slot], stage)
+
+            return act
 
         def span_of(j):
             return pl.ds((place // (1 << j)) * (1 << j), 1 << j)
 
-        chains = []
-        for n in range(2):
-            base = 2 * n * part
-            own = pl.multiple_of(base + tp * part, part)
-
-            def view(j, columns, base=base, own=own):
-                if columns is None and j == count - 1:
-                    return out_ref.at[span_of(j), :, pl.ds(base, 2 * part)]
-                return out_ref.at[span_of(j), :, pl.ds(own, part)]
-
-            chains.append(doubling(count, [(("tp", 0), count - 1, "own")], view, send))
-        for n in range(4, 8):
-            chains.append(
-                doubling(
-                    count, [], lambda j, _, n=n: out_ref.at[span_of(j), :, pl.ds(n * part, part)], send
-                )
-            )
-        small = doubling(count, [], lambda j, _: share_out.at[span_of(j)], send)
-        chains.append([(("share", 0), cost, start, end) for _, cost, start, end in small])
-        advance(chains)
+        def rows_view(j, start, size):
+            return lambda: out_ref.at[span_of(j), :, pl.ds(start, size)]
+
+        own = pl.multiple_of(tp * quarter, quarter)
+        crossing = [
+            hop("q", ("seq", count - 1 - j), rows_view(j, own, quarter)) for j in range(count - 1)
+        ]
+        crossing.append(hop("q", ("tp", 0), rows_view(count - 1, own, quarter)))
+        crossing.append(hop("q", ("seq", 0), rows_view(count - 1, 0, 2 * quarter)))
+        chains = [crossing]
+        for part in (2, 3):
+            chains.append([
+                hop(part, ("seq", count - 1 - j), rows_view(j, part * quarter, quarter))
+                for j in range(count)
+            ])
+        chains.append([
+            hop("s", ("seq", count - 1 - j), lambda j=j: share_out.at[span_of(j)])
+            for j in range(count)
+        ])
+        take_turns(chains)
+        for copy in flying.values():
+            copy.wait()
 
     return pl.pallas_call(
         kernel,
@@ -431,8 +437,9 @@
                     state["both"] = out
                     state["views"] = [out.at[h] for h in range(copies)]
 
-                price = {"z": 1.0 * size, "x": size, "c": 0.3 * size}[carrier(("seq", j))]
-                return (("seq", j), max(2.0, price) * copies, start, end)
+                price = {"z": 1.0 * size, "x": size, "c": 0.1 * size}[carrier(("seq", j))]
+                price = price if carrier(("seq", j)) != "z" else max(2.0, price)
+                return (("seq", j), price * copies, start, end)
 
             def tp_step():
                 size = blocks >> wide_at
@@ -643,8 +650,7 @@
     hidden = (resid.astype(f32) + moe_part).astype(bf16)
     last_hit = ((ends - 1)[:, None] == local_index[None, :]).astype(bf16)
     chosen = jnp.dot(last_hit, hidden, preferred_element_type=f32)
-    final = last_rows(chosen, final_gain, width)
-    log_probs = log_softmax(jnp.dot(final, w_head, preferred_element_type=f32))
+    log_probs = head_tail(chosen, final_gain, w_head, width)
     return (hidden, log_probs)
 
 

time: 316 us -> 317 us (level)
  local copies, waits for them, and re-layouts: 6.42 us -> 16.3 us
  matrix products: 31.4 us -> 25.5 us
  waiting for transfers between devices: 4.18 us -> 0.01 us
    unnamed x35 -> x40, local copies, waits for them, and re-layouts: 4.84 us -> 16 us
    dot_general x1 -> x0, matrix products: 5.26 us -> none  [on_device(): log_probs = log_softmax(jnp.dot(final, w_head, preferred_element_type=f32))]
    pallas_call x1, Pallas kernels: 68 us -> 72.7 us  [collect_rows(): pl.pallas_call(kernel, out_shape=jax.ShapeDtypeStruct((tall, half), jnp.f...]
    ppermute x4, waiting for transfers between devices: 4.18 us -> 0.01 us  [from_behind(): lax.ppermute(value, axis, [(source, source + steps) for source in range(l...]
    pallas_call x2 -> x1, Pallas kernels: 32.9 us -> 30.2 us  [head_tail(): pl.pallas_call(kernel, out_shape=jax.ShapeDtypeStruct((rows, vocab), f32)...]
  transfers between devices with their start and end apart: 4 -> 4, of which waited for: 1 -> 0; matrix products, arithmetic and copies ran while one was open for 4% -> 7% of each run, Pallas kernels for 0% -> 0%
where the time goes in v5:
time: 317 us; the launch traced here: 316 us
  Pallas kernels  241 us (76%)
  matrix products  25.5 us (8%)
  other arithmetic  20.1 us (6%)
  local copies, waits for them, and re-layouts  16.3 us (5%)
  starting transfers between devices  11.7 us (4%)
    pallas_call x1, Pallas kernels, spread_rows(): pl.pallas_call(kernel, out_shape=(jax.ShapeDtypeStruct((blocks, tall, wid...  78.8 us
    pallas_call x1, Pallas kernels, collect_rows(): pl.pallas_call(kernel, out_shape=jax.ShapeDtypeStruct((tall, half), jnp.f...  72.7 us
    pallas_call x1, Pallas kernels, gather_front(): pl.pallas_call(kernel, out_shape=tuple(shapes), in_specs=[pl.BlockSpec(me...  34.9 us
    pallas_call x1, Pallas kernels, head_tail(): pl.pallas_call(kernel, out_shape=jax.ShapeDtypeStruct((rows, vocab), f32)...  30.2 us
    unnamed x40, local copies, waits for them, and re-layouts  16 us
    pallas_call x1, Pallas kernels, sum_over_tp(): pl.pallas_call(kernel, out_shape=jax.ShapeDtypeStruct((rows, part), jnp.f...  15.9 us
    ppermute x4, starting transfers between devices, from_behind(): lax.ppermute(value, axis, [(source, source + steps) for source in range(l...  11.7 us
    pallas_call x1, Pallas kernels, attention(): pl.pallas_call(kernel, out_shape=jax.ShapeDtypeStruct((tall, wide), jnp.b...  8.98 us
  transfers between devices with their start and end apart: 4, of which 0 were waited for; matrix products, arithmetic and copies ran while one was open for 7% of the time, Pallas kernels for 0%

profile of v5, /device:TPU:0, one launch (start us, length us, event | category | flops | bytes accessed | tf_op | source)
XLA Modules:
  0.0 316.0 jit_solution(4701320453572780538)
XLA Ops:
  0.7 1.0 reduce-window.7
  1.7 1.2 broadcast_add_fusion
  2.8 0.7 convert_reduce_fusion
  3.5 0.5 copy-done.8
  4.0 1.3 select_reduce_fusion.2
  5.3 34.9 %gather_front.1 = (bf16[128,2048]{1,0:T(8,128)(2,1)}, bf16[16,32,1024]{2,1,0:T(8,128)(2,1)}, bf16[16,32,1024]{2,1,0:T(8,128)(2,1)}) custom-call(bf16[128,1024]{1,0:T(8,128)(2,1)} %block_ref.1, bf16[32,1024]{1,0:T(8,128)(2,1)} %rest_0_.1, bf16[32,1024]{1,0:T(8,128)(2,1)} %rest_1_.1), custom_call_target="tpu_custom_call" | custom-call | tf_op jit(solution)/shard_map/gather_front/pallas_call | solution.py:199
  40.2 1.4 fusion.7
  41.6 0.9 convert_element_type.82
  42.5 3.1 convolution_bitcast_fusion.1
  45.7 0.8 convolution_bitcast_fusion
  46.6 0.3 multiply_cosine_fusion
  46.9 1.2 subtract_convert_fusion
  48.1 0.1 pad_maximum_fusion.2
  48.3 0.5 copy-done.4
  48.8 0.8 convolution_convert_fusion.1
  49.6 3.1 collective-permute-start
  52.7 4.4 %collective-permute-start.1 = (bf16[128,2048]{1,0:T(8,128)(2,1)S(1)}, bf16[128,2048]{1,0:T(8,128)(2,1)}, u32[]{:S(2)}, u32[]{:S(2)}) collective-permute-start(bf16[128,2048]{1,0:T(8,128)(2,1)S(1)} %pad_maximum_fusion.rest_0_.rest_5_), channel_id=1, source_target_pairs={{0,4},{2,6},{4,8},{6,10},{8,12},{10,14},{12,16},{14,18},{16,20},{1... | collective-permute-start | bytes 1572872 | tf_op jit(solution)/shard_map/ppermute | solution.py:21
  57.1 2.1 collective-permute-start.2
  59.2 2.1 collective-permute-start.3
  61.3 0.5 broadcast_compare_fusion.2
  61.8 0.6 broadcast_compare_fusion
  62.8 0.7 compare_dynamic-update-slice_fusion
  63.5 0.8 and_dynamic-update-slice_fusion.4
  64.3 0.8 and_dynamic-update-slice_fusion.3
  65.1 0.7 and_dynamic-update-slice_fusion.2
  65.8 0.8 and_dynamic-update-slice_fusion.1
  66.6 0.8 and_dynamic-update-slice_fusion
  67.4 1.8 pad_maximum_fusion.1
  69.2 1.7 copy.34
  70.9 0.7 convert_element_type.98
  71.6 9.4 %copy.26.head_hbm = bf16[1024,3144]{1,0:T(8,128)(2,1)} copy(bf16[1024,3144]{0,1:T(8,128)(2,1)} %param.37) | data formatting | bytes 12877824 | tf_op args[18]
  81.0 0.9 broadcast_select_fusion.bias_ref
  81.9 9.0 %attention.1 = bf16[128,1024]{1,0:T(8,128)(2,1)} custom-call(bf16[128,1024]{1,0:T(8,128)(2,1)} %bitcast.51, bf16[512,1024]{1,0:T(8,128)(2,1)} %bitcast.55, bf16[512,1024]{1,0:T(8,128)(2,1)} %bitcast.56, f32[128,1152]{1,0:T(8,128)} %broadcast_select_fusion.bias_ref, bf16[128,2048]{1,0:T(8,128)(2,1)} %copy-done.3, ...), custom_call_target="tpu_custom_call" | custom-call | flops 603979776 | bytes 4718592 | tf_op jit(solution)/shard_map/attention/pallas_call | solution.py:515
  91.0 3.8 %convolution_convert_fusion.block_ref = bf16[128,2048]{1,0:T(8,128)(2,1)} fusion(bf16[128,1024]{1,0:T(8,128)(2,1)} %attention.1, bf16[1024,2048]{1,0:T(8,128)(2,1)} %param.24), kind=kOutput, calls=%fused_computation.2 | convolution fusion | flops 537133056 | bytes 4980736 | tf_op jit(solution)/shard_map/dot_general | solution.py:604
  94.8 15.9 %sum_over_tp.1 = f32[128,2048]{1,0:T(8,128)} custom-call(bf16[128,2048]{1,0:T(8,128)(2,1)} %convolution_convert_fusion.block_ref), custom_call_target="tpu_custom_call" | custom-call | tf_op jit(solution)/shard_map/sum_over_tp/pallas_call | solution.py:226
  110.7 1.6 fusion.4
  112.3 0.2 fusion.6.rows_ref
  112.5 0.3 fusion.24
  112.8 78.8 %spread_rows.1 = (bf16[16,128,2048]{2,1,0:T(8,128)(2,1)S(1)}, f32[16,16,128]{2,1,0:T(8,128)S(1)}) custom-call(bf16[128,2048]{1,0:T(8,128)(2,1)S(1)} %fusion.6.rows_ref, f32[16,128]{1,0:T(8,128)S(1)} %bitcast.45), custom_call_target="tpu_custom_call" | custom-call | tf_op jit(solution)/shard_map/spread_rows/pallas_call | solution.py:357
  191.7 4.6 %fusion.2 = f32[2048,512]{1,0:T(8,128)S(1)} fusion(bf16[2048,2048]{1,0:T(8,128)(2,1)S(1)} %bitcast.46, bf16[1,2048,512]{2,1,0:T(8,128)(2,1)S(1)} %copy-done.15), kind=kOutput, calls=%fused_computation.5 | convolution fusion | flops 4294967296 | bytes 14680064 | tf_op jit(solution)/shard_map/dot_general | solution.py:617
  196.3 5.2 %multiply_convert_fusion.1 = bf16[2048,512]{1,0:T(8,128)(2,1)S(1)} fusion(f32[2048,512]{1,0:T(8,128)S(1)} %fusion.2, bf16[2048,2048]{1,0:T(8,128)(2,1)S(1)} %bitcast.47, bf16[1,2048,512]{2,1,0:T(8,128)(2,1)S(1)} %copy-done.16), kind=kOutput, calls=%fused_computation.1 | convolution fusion | flops 4301258752 | bytes 16777216 | tf_op jit(solution)/shard_map/dot_general | solution.py:618
  201.5 6.8 %multiply_convert_fusion = bf16[2048,2048]{1,0:T(8,128)(2,1)} fusion(bf16[2048,512]{1,0:T(8,128)(2,1)S(1)} %multiply_convert_fusion.1, f32[2048]{0:T(1024)S(1)} %bitcast.58, bf16[1,512,2048]{2,1,0:T(8,128)(2,1)S(1)} %copy-done), kind=kOutput, calls=%fused_computation | convolution fusion | flops 4303355904 | bytes 12591104 | tf_op jit(solution)/shard_map/dot_general | solution.py:620
  208.3 72.7 %collect_rows.1 = f32[128,1024]{1,0:T(8,128)} custom-call(bf16[16,128,2048]{2,1,0:T(8,128)(2,1)} %bitcast.48), custom_call_target="tpu_custom_call" | custom-call | tf_op jit(solution)/shard_map/collect_rows/pallas_call | solution.py:469
  281.0 1.1 add_convert_fusion
  282.1 0.2 fusion.13.chosen_ref
  282.3 2.9 copy-done.1
  285.2 30.2 %head_tail.1 = f32[8,3144]{1,0:T(8,128)S(1)} custom-call(f32[8,1024]{1,0:T(8,128)S(1)} %fusion.13.chosen_ref, bf16[1,1024]{1,0:T(2,128)(2,1)S(1)} %reshape.217.gain_ref, bf16[1024,3144]{1,0:T(8,128)(2,1)S(1)} %copy-done.1), custom_call_target="tpu_custom_call" | custom-call | tf_op jit(solution)/shard_map/head_tail/pallas_call | solution.py:128
  315.4 0.6 copy.41
  (56 shorter events, 0.9 us)
Async XLA Ops:
  0.6 200.9 %copy-start = (bf16[1,512,2048]{2,1,0:T(8,128)(2,1)S(1)}, bf16[1,512,2048]{2,1,0:T(8,128)(2,1)}, u32[]{:S(2)}) copy-start(bf16[1,512,2048]{2,1,0:T(8,128)(2,1)} %param.34) | copy-start | bytes 6291460
  0.7 4.6 %copy-start.9 = (s32[128]{0:T(128)}, s32[128]{0:T(128)S(1)}, u32[]{:S(2)}) copy-start(s32[128]{0:T(128)S(1)} %iota_add_fusion.4) | copy-start | bytes 1540
  3.5 0.5 copy-start.8
  40.2 5.5 %copy-start.2 = (bf16[128,2048]{1,0:T(8,128)(2,1)S(1)}, bf16[128,2048]{1,0:T(8,128)(2,1)}, u32[]{:S(2)}) copy-start(bf16[128,2048]{1,0:T(8,128)(2,1)} %get-tuple-element.7) | copy-start | bytes 1572868
  40.2 5.5 %copy-start.5 = (bf16[2048,1024]{1,0:T(8,128)(2,1)S(1)}, bf16[2048,1024]{1,0:T(8,128)(2,1)}, u32[]{:S(2)}) copy-start(bf16[2048,1024]{1,0:T(8,128)(2,1)} %param.22) | copy-start | bytes 12582916
  46.5 2.3 copy-start.4
  48.1 14.3 %copy-start.14 = (s32[16]{0:T(128)S(1)}, s32[16]{0:T(128)}, u32[]{:S(2)}) copy-start(s32[16]{0:T(128)} %param.27) | copy-start | bytes 196
  49.6 31.4 %copy-start.3 = (bf16[128,2048]{1,0:T(8,128)(2,1)}, bf16[128,2048]{1,0:T(8,128)(2,1)S(1)}, u32[]{:S(2)}) copy-start(bf16[128,2048]{1,0:T(8,128)(2,1)S(1)} %pad_maximum_fusion.rest_0_.rest_5_) | copy-start | bytes 1572868
  49.6 32.3 %collective-permute-start = (bf16[128,2048]{1,0:T(8,128)(2,1)S(1)}, bf16[128,2048]{1,0:T(8,128)(2,1)}, u32[]{:S(2)}, u32[]{:S(2)}) collective-permute-start(bf16[128,2048]{1,0:T(8,128)(2,1)S(1)} %pad_maximum_fusion.rest_0_.rest_5_), channel_id=1, source_target_pairs={{0,2},{2,4},{4,6},{6,8},{8,10},{10,12},{12,14},{14,16},{16,18},{18... | collective-permute-start | bytes 1572872 | tf_op jit(solution)/shard_map/ppermute | solution.py:21
  52.7 29.2 %collective-permute-start.1 = (bf16[128,2048]{1,0:T(8,128)(2,1)S(1)}, bf16[128,2048]{1,0:T(8,128)(2,1)}, u32[]{:S(2)}, u32[]{:S(2)}) collective-permute-start(bf16[128,2048]{1,0:T(8,128)(2,1)S(1)} %pad_maximum_fusion.rest_0_.rest_5_), channel_id=1, source_target_pairs={{0,4},{2,6},{4,8},{6,10},{8,12},{10,14},{12,16},{14,18},{16,20},{1... | collective-permute-start | bytes 1572872 | tf_op jit(solution)/shard_map/ppermute | solution.py:21
  57.1 24.8 %collective-permute-start.2 = (bf16[128,2048]{1,0:T(8,128)(2,1)S(1)}, bf16[128,2048]{1,0:T(8,128)(2,1)}, u32[]{:S(2)}, u32[]{:S(2)}) collective-permute-start(bf16[128,2048]{1,0:T(8,128)(2,1)S(1)} %pad_maximum_fusion.rest_0_.rest_5_), channel_id=1, source_target_pairs={{0,6},{2,8},{4,10},{6,12},{8,14},{10,16},{12,18},{14,20},{16,22},{... | collective-permute-start | bytes 1572872 | tf_op jit(solution)/shard_map/ppermute | solution.py:21
  59.2 22.7 %collective-permute-start.3 = (bf16[128,2048]{1,0:T(8,128)(2,1)S(1)}, bf16[128,2048]{1,0:T(8,128)(2,1)}, u32[]{:S(2)}, u32[]{:S(2)}) collective-permute-start(bf16[128,2048]{1,0:T(8,128)(2,1)S(1)} %pad_maximum_fusion.rest_0_.rest_5_), channel_id=1, source_target_pairs={{0,8},{2,10},{4,12},{6,14},{8,16},{10,18},{12,20},{14,22},{16,24},... | collective-permute-start | bytes 1572872 | tf_op jit(solution)/shard_map/ppermute | solution.py:21
  71.6 9.5 %copy-start.13 = (bf16[1024]{0:T(1024)(128)(2,1)S(1)}, bf16[1024]{0:T(1024)(128)(2,1)}, u32[]{:S(2)}) copy-start(bf16[1024]{0:T(1024)(128)(2,1)} %param.36) | copy-start | bytes 6148
  90.9 21.6 %copy-start.7 = (bf16[2048,16]{0,1:T(8,128)(2,1)S(1)}, bf16[2048,16]{0,1:T(8,128)(2,1)}, u32[]{:S(2)}) copy-start(bf16[2048,16]{0,1:T(8,128)(2,1)} %param.31) | copy-start | bytes 196612
  90.9 21.9 %copy-start.11 = (s32[128,8]{0,1:T(8,128)S(1)}, s32[128,8]{0,1:T(8,128)}, u32[]{:S(2)}) copy-start(s32[128,8]{0,1:T(8,128)} %param.35) | copy-start | bytes 12292
  110.7 81.0 %copy-start.15 = (bf16[1,2048,512]{2,1,0:T(8,128)(2,1)S(1)}, bf16[1,2048,512]{2,1,0:T(8,128)(2,1)}, u32[]{:S(2)}) copy-start(bf16[1,2048,512]{2,1,0:T(8,128)(2,1)} %param.32) | copy-start | bytes 6291460
  191.7 4.6 %copy-start.16 = (bf16[1,2048,512]{2,1,0:T(8,128)(2,1)S(1)}, bf16[1,2048,512]{2,1,0:T(8,128)(2,1)}, u32[]{:S(2)}) copy-start(bf16[1,2048,512]{2,1,0:T(8,128)(2,1)} %param.33) | copy-start | bytes 6291460
  208.3 73.8 %copy-start.10 = (s32[128]{0:T(128)S(1)}, s32[128]{0:T(128)}, u32[]{:S(2)}) copy-start(s32[128]{0:T(128)} %copy-done.9) | copy-start | bytes 1540
  208.3 73.8 %copy-start.12 = (s32[8]{0:T(128)S(1)}, s32[8]{0:T(128)}, u32[]{:S(2)}) copy-start(s32[8]{0:T(128)} %get-tuple-element.29) | copy-start | bytes 100
  282.1 33.9 %copy-start.6 = (bf16[128,1024]{1,0:T(8,128)(2,1)}, bf16[128,1024]{1,0:T(8,128)(2,1)S(1)}, u32[]{:S(2)}) copy-start(bf16[128,1024]{1,0:T(8,128)(2,1)S(1)} %add_convert_fusion) | copy-start | bytes 786436
  282.3 2.9 copy-start.1
